TPU v7x, 256 devices: a whole 4x4x8 slice. The times are simulated.
256 devices in a mesh: qrow: 16 (over x, y_hi, core), kcol: 16 (over y_lo, z).
Axes of the slice: x: 4, y: 4 (y_hi: 2, y_lo: 2; y = y_hi * 2 + y_lo), z: 8, core: 2. Of those that a mesh axis runs over, the one named last changes fastest.
Arguments:
- query_states: bfloat16 [32768, 512], P(('qrow', 'kcol')), may hold values from -8 to 8
- key_states: bfloat16 [32768, 512], P(('kcol', 'qrow')), may hold values from -8 to 8
- value_states: bfloat16 [32768, 512], P(('kcol', 'qrow')), may hold values from -6 to 6
- saved_output: bfloat16 [32768, 512], P(('qrow', 'kcol')), may hold values from -0.59765625 to 0.59765625
- output_grad: bfloat16 [32768, 512], P(('qrow', 'kcol')), may hold values from -6 to 6
- normalizer: float32 [32768, 4], P(('qrow', 'kcol')), as said below
- doc_lengths: int32 [8], replicated, may hold values from 1 to 8192, as said below
Outputs:
- query_grad: bfloat16 [32768, 512], P(('qrow', 'kcol'))
- key_grad: bfloat16 [32768, 512], P(('kcol', 'qrow'))
- value_grad: bfloat16 [32768, 512], P(('kcol', 'qrow'))
Inputs may be any that keep to these rules, and one draw needn't show every extreme that they name: `doc_lengths`: the 8 lengths sum to 32768; exactly one of them equals 8192, every other one is smaller. normalizer[p, h] is the logarithm of the sum of exp(scores[h, p, t]) over the t that allowed admits, computed in float32 from query_states, key_states and doc_lengths.
All inputs are finite; a program needn't handle non-finite values.
Results may differ from a plain program's by a relative error of at most 0.005.
Values may be sent and summed in bfloat16 or wider, within the bound.
No kernel may reach another device: no remote copies, remote signals or barrier semaphores. Data moves between devices by JAX's collectives and lax.ppermute only.
A program may use at most 192 MiB of HBM per device.

v0:
```python
import jax
import jax.numpy as jnp
from jax import lax
from jax.sharding import Mesh
from jax.sharding import PartitionSpec as P

HEAD_DIM = 128
KV_HEADS = 4
GROUP = 1
TILES = 8
KCOL = ("kcol_0", "kcol_1")
QROW_KCOL = ("qrow", "kcol_0", "kcol_1")
KCOL_QROW = ("kcol_0", "kcol_1", "qrow")


def side_by_side(arrays, axis, dim, along):
    widths = [a.shape[along] for a in arrays]
    both = jnp.concatenate(arrays, axis=along)
    filled = lax.all_gather(both, axis, axis=dim, tiled=True)
    return tuple(jnp.split(filled, [sum(widths[:k]) for k in range(1, len(widths))], axis=along))


def reduced_to_own(pieces, axes, order):
    inside = pieces.shape[1:]
    pieces = pieces.reshape(*(lax.axis_size(a) for a in axes), *inside)
    pieces = jnp.moveaxis(pieces, order, range(len(axes))).reshape(-1, *inside)
    for k in order:
        pieces = lax.psum_scatter(pieces, axes[k], scatter_dimension=0, tiled=True)
    return pieces[0]


def cut_along(x, dim, length):
    before, after = (x.shape[:dim], x.shape[dim + 1 :])
    return jnp.moveaxis(x.reshape(*before, length, -1, *after), dim, 0)


def summed_rows(x, axes, order, dim):
    length = lax.axis_size(axes)
    return reduced_to_own(cut_along(x, dim, length), axes, order)


def side_by_side_2(arrays, axis, dim, along):
    ends, at = ([], 0)
    for a in arrays[:-1]:
        at += a.shape[along]
        ends.append(at)
    both = jnp.concatenate(arrays, axis=along)
    return tuple(
        jnp.split(lax.psum_scatter(both, axis, scatter_dimension=dim, tiled=True), ends, axis=along)
    )


def document_ids(doc_lengths, positions):
    doc_ends = jnp.cumsum(doc_lengths)
    return jnp.sum((positions[:, None] >= doc_ends[None, :]).astype(jnp.int32), axis=1)


def add_tile(running, query_tile, grad_tile, norm_tile, delta_tile, key_tile, value_tile, allowed):
    query_acc, key_acc, value_acc = running
    query_count = query_tile.shape[0]
    key_count = key_tile.shape[0]
    scaling = HEAD_DIM ** (-0.5)
    query_heads = query_tile.reshape(query_count, KV_HEADS, GROUP, HEAD_DIM)
    grad_heads = grad_tile.reshape(query_count, KV_HEADS, GROUP, HEAD_DIM)
    key_heads = key_tile.reshape(key_count, KV_HEADS, HEAD_DIM)
    value_heads = value_tile.reshape(key_count, KV_HEADS, HEAD_DIM)
    norm_heads = norm_tile.reshape(query_count, KV_HEADS, GROUP).transpose(1, 2, 0)[..., None]
    delta_heads = delta_tile.reshape(query_count, KV_HEADS, GROUP).transpose(1, 2, 0)[..., None]
    scores = (
        jnp.einsum("qhgd,khd->hgqk", query_heads, key_heads, preferred_element_type=jnp.float32)
        * scaling
    )
    probability = jnp.where(allowed[None, None], jnp.exp(scores - norm_heads), 0.0)
    prob_grad = jnp.einsum(
        "qhgd,khd->hgqk", grad_heads, value_heads, preferred_element_type=jnp.float32
    )
    score_grad = probability * (prob_grad - delta_heads)
    prob_half = probability.astype(jnp.bfloat16)
    grad_half = score_grad.astype(jnp.bfloat16)
    value_add = jnp.einsum(
        "hgqk,qhgd->khd", prob_half, grad_heads, preferred_element_type=jnp.float32
    )
    key_add = jnp.einsum(
        "hgqk,qhgd->khd", grad_half, query_heads, preferred_element_type=jnp.float32
    )
    query_add = jnp.einsum(
        "hgqk,khd->qhgd", grad_half, key_heads, preferred_element_type=jnp.float32
    )
    return (
        query_acc + query_add.reshape(query_count, KV_HEADS * GROUP * HEAD_DIM),
        key_acc + key_add.reshape(key_count, KV_HEADS * HEAD_DIM),
        value_acc + value_add.reshape(key_count, KV_HEADS * HEAD_DIM),
    )


def run_tile(running, operands):
    return add_tile(running, *operands)


def per_device(
    query_states, key_states, value_states, saved_output, output_grad, normalizer, doc_lengths
):
    row_index = lax.axis_index("qrow")
    col_index = lax.axis_index(KCOL)
    head_count = KV_HEADS * GROUP
    scaling = HEAD_DIM ** (-0.5)
    local_rows = query_states.shape[0]
    row_delta = jnp.sum(
        (output_grad.astype(jnp.float32) * saved_output.astype(jnp.float32)).reshape(
            local_rows, head_count, HEAD_DIM
        ),
        axis=2,
    )
    query_block, grad_block = side_by_side((query_states, output_grad), KCOL, 0, 1)
    norm_block, delta_block = side_by_side((normalizer, row_delta), KCOL, 0, 1)
    key_block, value_block = side_by_side((key_states, value_states), "qrow", 0, 1)
    query_len = query_block.shape[0]
    key_len = key_block.shape[0]
    query_iota = jnp.arange(query_len, dtype=jnp.int32)
    key_iota = jnp.arange(key_len, dtype=jnp.int32)
    query_pos = row_index * query_len + query_iota
    key_pos = col_index * key_len + key_iota
    query_doc = document_ids(doc_lengths, query_pos)
    key_doc = document_ids(doc_lengths, key_pos)
    tile_query = query_len // TILES
    tile_key = key_len // TILES
    key_accs = [
        jnp.zeros((tile_key, KV_HEADS * HEAD_DIM), jnp.float32) for key_step in range(TILES)
    ]
    value_accs = [
        jnp.zeros((tile_key, KV_HEADS * HEAD_DIM), jnp.float32) for key_step in range(TILES)
    ]
    query_parts = []
    for query_step in range(TILES):
        query_lo = query_step * tile_query
        query_hi = query_lo + tile_query
        query_acc = jnp.zeros((tile_query, head_count * HEAD_DIM), jnp.float32)
        for key_step in range(TILES):
            key_lo = key_step * tile_key
            key_hi = key_lo + tile_key
            allowed = (key_pos[key_lo:key_hi][None, :] <= query_pos[query_lo:query_hi][:, None]) & (
                key_doc[key_lo:key_hi][None, :] == query_doc[query_lo:query_hi][:, None]
            )
            operands = (
                query_block[query_lo:query_hi],
                grad_block[query_lo:query_hi],
                norm_block[query_lo:query_hi],
                delta_block[query_lo:query_hi],
                key_block[key_lo:key_hi],
                value_block[key_lo:key_hi],
                allowed,
            )
            running = (query_acc, key_accs[key_step], value_accs[key_step])
            running = run_tile(running, operands)
            query_acc, key_accs[key_step], value_accs[key_step] = running
        query_parts.append(query_acc)
    query_total = jnp.concatenate(query_parts, axis=0) * scaling
    key_total = jnp.concatenate(key_accs, axis=0) * scaling
    value_total = jnp.concatenate(value_accs, axis=0)
    query_grad = summed_rows(query_total, KCOL, (1, 0), 0)
    key_grad, value_grad = side_by_side_2((key_total, value_total), "qrow", 0, 1)
    return (
        query_grad.astype(jnp.bfloat16),
        key_grad.astype(jnp.bfloat16),
        value_grad.astype(jnp.bfloat16),
    )


def solution(mesh):
    finer = Mesh(mesh.devices.reshape(mesh.shape["qrow"], 2, 8), ("qrow", "kcol_0", "kcol_1"))
    return jax.shard_map(
        per_device,
        mesh=finer,
        in_specs=(
            P(QROW_KCOL, None),
            P(KCOL_QROW, None),
            P(KCOL_QROW, None),
            P(QROW_KCOL, None),
            P(QROW_KCOL, None),
            P(QROW_KCOL, None),
            P(),
        ),
        out_specs=(P(QROW_KCOL, None), P(KCOL_QROW, None), P(KCOL_QROW, None)),
        check_vma=False,
    )
```

profile of v0, /device:TPU:40, one launch (start us, length us, event | category | flops | bytes accessed | tf_op | source)
XLA Modules:
  0.0 651.2 jit_solution(9195269231096992289)
XLA Ops:
  15.9 32.5 %all_gather.11 = f32[2048,8]{0,1:T(8,128)S(1)} all-gather(f32[128,8]{0,1:T(8,128)S(1)} %pad_maximum_fusion.3), channel_id=1, replica_groups=mesh['qrow'=16,'kcol_0'=2,'kcol_1'=8] {'kcol_0','kcol_1'}, dimensions={0}, use_global_device_ids=true | all-gather | bytes 69632 | tf_op jit(solution)/shard_map/all_gather | solution.py:19
  52.3 2.2 compare_and_fusion.2
  54.5 2.4 compare_and_fusion
  56.9 19.5 %all-gather.3.cloned.1.call-done = bf16[2048,1024]{0,1:T(8,128)(2,1)} async-done(((bf16[128,1024]{0,1:T(8,128)(2,1)}), bf16[2048,1024]{0,1:T(8,128)(2,1)}) %all-gather.3.cloned.1.call-update) | async-done | bytes 4194320 | tf_op jit(solution)/shard_map/all_gather | solution.py:19
  76.4 4.3 fusion.777
  80.6 84.5 %all-gather.5.cloned.1.call-done = bf16[2048,1024]{0,1:T(8,128)(2,1)} async-done(((bf16[128,1024]{0,1:T(8,128)(2,1)}), bf16[2048,1024]{0,1:T(8,128)(2,1)}) %all-gather.5.cloned.1.call-update) | async-done | bytes 4194320 | tf_op jit(solution)/shard_map/all_gather | solution.py:19
  165.2 3.3 fusion.776
  207.5 2.0 copy.2193
  211.0 2.3 fusion.611
  223.1 2.0 copy.2196
  234.6 2.1 copy.2197
  291.1 2.1 copy.2266
  293.2 2.0 copy.2338
  302.9 2.1 copy.2271
  326.7 2.1 copy.2269
  328.8 2.0 copy.2341
  333.3 2.2 fusion.639
  348.7 2.1 copy.2194
  370.7 2.0 copy.2339
  399.3 2.0 copy.2200
  409.8 2.1 copy.2273
  422.6 2.1 copy.2199
  430.8 2.1 copy.2272
  439.8 2.0 copy.2198
  447.0 2.8 copy.2201
  456.0 2.0 copy.2344
  475.8 2.2 copy.2340
  492.6 12.1 %reduce-scatter.4.cloned.1.call-done = f32[2,128,512]{2,1,0:T(8,128)} async-done(((f32[16,128,512]{2,1,0:T(8,128)}), f32[2,128,512]{2,1,0:T(8,128)}) %reduce-scatter.4.cloned.1.call-update) | async-done | bytes 524304 | tf_op jit(solution)/shard_map/reduce_scatter | solution.py:28
  504.7 2.7 broadcast_multiply_fusion
  507.4 7.0 %pad_maximum_fusion = f32[2048,1024]{1,0:T(8,128)} fusion(f32[2048,512]{1,0:T(8,128)} %constant_dynamic-update-slice_fusion.16, f32[2048,512]{1,0:T(8,128)S(1)} %broadcast_multiply_fusion), kind=kLoop, calls=%fused_computation | loop fusion | flops 2097152 | bytes 16777216 | tf_op jit(solution)/shard_map/concatenate | solution.py:47
  514.5 11.7 %reduce-scatter.6.cloned.1.call-done = f32[1,128,512]{2,1,0:T(8,128)} async-done(((f32[2,128,512]{2,1,0:T(8,128)}), f32[1,128,512]{2,1,0:T(8,128)}) %reduce-scatter.6.cloned.1.call-update) | async-done | bytes 262160 | tf_op jit(solution)/shard_map/reduce_scatter | solution.py:28
  527.7 114.9 %reduce-scatter.8.cloned.1.call-done = f32[128,1024]{1,0:T(8,128)} async-done(((f32[2048,1024]{1,0:T(8,128)}), f32[128,1024]{1,0:T(8,128)}) %reduce-scatter.8.cloned.1.call-update) | async-done | bytes 524304 | tf_op jit(solution)/shard_map/reduce_scatter | solution.py:49
  (1065 shorter events, 291.9 us)
Async XLA Ops:
  7.2 69.2 %all-gather.3.cloned.1.call-start = ((), (), s32[]{:S(2)}) async-start(), calls=%async_computation.3 | async-start | bytes 4456448 | tf_op jit(solution)/shard_map/all_gather | solution.py:19
  10.0 155.2 %all-gather.5.cloned.1.call-start = ((), (), s32[]{:S(2)}) async-start(), calls=%async_computation.4 | async-start | bytes 4456448 | tf_op jit(solution)/shard_map/all_gather | solution.py:19
  12.9 491.7 %reduce-scatter.4.cloned.1.call-start = ((), (), s32[]{:S(2)}) async-start(), calls=%async_computation.5 | async-start | bytes 4718592 | tf_op jit(solution)/shard_map/reduce_scatter | solution.py:28
  168.5 35.2 %copy-start = (bf16[256,512]{0,1:T(8,128)(2,1)}, bf16[256,512]{0,1:T(8,128)(2,1)S(1)}, u32[]{:S(2)}) copy-start(bf16[256,512]{0,1:T(8,128)(2,1)S(1)} %get-tuple-element.19) | copy-start | bytes 786436
  168.5 35.5 %copy-start.4 = (bf16[256,512]{0,1:T(8,128)(2,1)}, bf16[256,512]{0,1:T(8,128)(2,1)S(1)}, u32[]{:S(2)}) copy-start(bf16[256,512]{0,1:T(8,128)(2,1)S(1)} %get-tuple-element.20) | copy-start | bytes 786436
  179.7 25.5 %copy-start.167 = (bf16[4,256,256]{1,2,0:T(8,128)(2,1)}, bf16[4,256,256]{1,2,0:T(8,128)(2,1)S(1)}, u32[]{:S(2)}) copy-start(bf16[4,256,256]{1,2,0:T(8,128)(2,1)S(1)} %fusion.578) | copy-start | bytes 1572868
  240.0 27.8 %copy-start.130 = (bf16[4,256,256]{1,2,0:T(8,128)(2,1)}, bf16[4,256,256]{1,2,0:T(8,128)(2,1)S(1)}, u32[]{:S(2)}) copy-start(bf16[4,256,256]{1,2,0:T(8,128)(2,1)S(1)} %fusion.589) | copy-start | bytes 1572868
  240.9 21.4 %copy-start.132 = (bf16[4,256,256]{1,2,0:T(8,128)(2,1)}, bf16[4,256,256]{1,2,0:T(8,128)(2,1)S(1)}, u32[]{:S(2)}) copy-start(bf16[4,256,256]{1,2,0:T(8,128)(2,1)S(1)} %fusion.588) | copy-start | bytes 1572868
  242.1 31.4 %copy-start.134 = (bf16[4,256,256]{1,2,0:T(8,128)(2,1)}, bf16[4,256,256]{1,2,0:T(8,128)(2,1)S(1)}, u32[]{:S(2)}) copy-start(bf16[4,256,256]{1,2,0:T(8,128)(2,1)S(1)} %fusion.587) | copy-start | bytes 1572868
  288.4 6.9 %copy-start.324 = (pred[256,256]{0,1:T(8,128)(4,1)S(1)}, pred[256,256]{0,1:T(8,128)(4,1)}, u32[]{:S(2)}) copy-start(pred[256,256]{0,1:T(8,128)(4,1)} %get-tuple-element.126) | copy-start | bytes 196612
  325.6 9.8 %copy-start.321 = (pred[256,256]{0,1:T(8,128)(4,1)S(1)}, pred[256,256]{0,1:T(8,128)(4,1)}, u32[]{:S(2)}) copy-start(pred[256,256]{0,1:T(8,128)(4,1)} %get-tuple-element.88) | copy-start | bytes 196612
  346.5 7.0 %copy-start.317 = (pred[256,256]{0,1:T(8,128)(4,1)S(1)}, pred[256,256]{0,1:T(8,128)(4,1)}, u32[]{:S(2)}) copy-start(pred[256,256]{0,1:T(8,128)(4,1)} %get-tuple-element.91) | copy-start | bytes 196612
  348.7 6.7 %copy-start.316 = (pred[256,256]{0,1:T(8,128)(4,1)S(1)}, pred[256,256]{0,1:T(8,128)(4,1)}, u32[]{:S(2)}) copy-start(pred[256,256]{0,1:T(8,128)(4,1)} %get-tuple-element.105) | copy-start | bytes 196612
  366.1 6.6 %copy-start.314 = (pred[256,256]{0,1:T(8,128)(4,1)S(1)}, pred[256,256]{0,1:T(8,128)(4,1)}, u32[]{:S(2)}) copy-start(pred[256,256]{0,1:T(8,128)(4,1)} %get-tuple-element.98) | copy-start | bytes 196612
  387.1 7.2 %copy-start.310 = (pred[256,256]{0,1:T(8,128)(4,1)S(1)}, pred[256,256]{0,1:T(8,128)(4,1)}, u32[]{:S(2)}) copy-start(pred[256,256]{0,1:T(8,128)(4,1)} %get-tuple-element.102) | copy-start | bytes 196612
  408.7 9.1 %copy-start.306 = (pred[256,256]{0,1:T(8,128)(4,1)S(1)}, pred[256,256]{0,1:T(8,128)(4,1)}, u32[]{:S(2)}) copy-start(pred[256,256]{0,1:T(8,128)(4,1)} %get-tuple-element.100) | copy-start | bytes 196612
  426.2 6.7 %copy-start.304 = (pred[256,256]{0,1:T(8,128)(4,1)S(1)}, pred[256,256]{0,1:T(8,128)(4,1)}, u32[]{:S(2)}) copy-start(pred[256,256]{0,1:T(8,128)(4,1)} %get-tuple-element.103) | copy-start | bytes 196612
  449.8 76.3 %reduce-scatter.6.cloned.1.call-start = ((), (), s32[]{:S(2)}) async-start(), calls=%async_computation.6 | async-start | bytes 786432 | tf_op jit(solution)/shard_map/reduce_scatter | solution.py:28
  467.0 6.6 %copy-start.174 = (f32[4,1,256,256]{2,3,0,1:T(8,128)S(1)}, f32[4,1,256,256]{2,3,0,1:T(8,128)}, u32[]{:S(2)}) copy-start(f32[4,1,256,256]{2,3,0,1:T(8,128)} %copy-done.173) | copy-start | bytes 3145732
  474.6 8.6 %copy-start.264 = (f32[256,512]{1,0:T(8,128)S(1)}, f32[256,512]{1,0:T(8,128)}, u32[]{:S(2)}) copy-start(f32[256,512]{1,0:T(8,128)} %copy.2342) | copy-start | bytes 1572868
  475.8 6.6 %copy-start.266 = (f32[256,512]{1,0:T(8,128)S(1)}, f32[256,512]{1,0:T(8,128)}, u32[]{:S(2)}) copy-start(f32[256,512]{1,0:T(8,128)} %copy.2341) | copy-start | bytes 1572868
  475.8 8.3 %copy-start.262 = (f32[256,512]{1,0:T(8,128)S(1)}, f32[256,512]{1,0:T(8,128)}, u32[]{:S(2)}) copy-start(f32[256,512]{1,0:T(8,128)} %copy.2343) | copy-start | bytes 1572868
  477.9 7.0 %copy-start.278 = (f32[256,512]{1,0:T(8,128)S(1)}, f32[256,512]{1,0:T(8,128)}, u32[]{:S(2)}) copy-start(f32[256,512]{1,0:T(8,128)} %copy.2344) | copy-start | bytes 1572868
  477.9 7.9 %copy-start.272 = (f32[256,512]{1,0:T(8,128)S(1)}, f32[256,512]{1,0:T(8,128)}, u32[]{:S(2)}) copy-start(f32[256,512]{1,0:T(8,128)} %copy.2345) | copy-start | bytes 1572868
  478.8 7.9 %copy-start.269 = (f32[256,512]{1,0:T(8,128)S(1)}, f32[256,512]{1,0:T(8,128)}, u32[]{:S(2)}) copy-start(f32[256,512]{1,0:T(8,128)} %copy.2267) | copy-start | bytes 1572868
  479.6 7.9 %copy-start.280 = (f32[256,512]{1,0:T(8,128)S(1)}, f32[256,512]{1,0:T(8,128)}, u32[]{:S(2)}) copy-start(f32[256,512]{1,0:T(8,128)} %copy.2268) | copy-start | bytes 1572868
  480.5 7.9 %copy-start.265 = (f32[256,512]{1,0:T(8,128)S(1)}, f32[256,512]{1,0:T(8,128)}, u32[]{:S(2)}) copy-start(f32[256,512]{1,0:T(8,128)} %copy.2269) | copy-start | bytes 1572868
  482.4 6.8 %copy-start.263 = (f32[256,512]{1,0:T(8,128)S(1)}, f32[256,512]{1,0:T(8,128)}, u32[]{:S(2)}) copy-start(f32[256,512]{1,0:T(8,128)} %copy.2270) | copy-start | bytes 1572868
  483.3 6.8 %copy-start.259 = (f32[256,512]{1,0:T(8,128)S(1)}, f32[256,512]{1,0:T(8,128)}, u32[]{:S(2)}) copy-start(f32[256,512]{1,0:T(8,128)} %copy.2271) | copy-start | bytes 1572868
  484.1 6.8 %copy-start.273 = (f32[256,512]{1,0:T(8,128)S(1)}, f32[256,512]{1,0:T(8,128)}, u32[]{:S(2)}) copy-start(f32[256,512]{1,0:T(8,128)} %copy.2272) | copy-start | bytes 1572868
  485.0 6.8 %copy-start.271 = (f32[256,512]{1,0:T(8,128)S(1)}, f32[256,512]{1,0:T(8,128)}, u32[]{:S(2)}) copy-start(f32[256,512]{1,0:T(8,128)} %copy.2273) | copy-start | bytes 1572868
  504.7 137.9 %reduce-scatter.8.cloned.1.call-start = ((), (), s32[]{:S(2)}) async-start(), calls=%async_computation.7 | async-start | bytes 8912896 | tf_op jit(solution)/shard_map/reduce_scatter | solution.py:49
  (314 other events, 1007.8 us)
Sparse Core Ops, SparseCore 0:
  10.5 65.7 all-gather.2
  78.1 87.0 all-gather.4
  449.9 54.6 reduce-scatter.3
  507.0 19.0 reduce-scatter.5
  531.3 111.2 reduce-scatter.7
where the time goes:
time: 659 us; the launch traced here: 651 us
  waiting for transfers between devices  243 us (37%)
  matrix products  237 us (36%)
  local copies, waits for them, and re-layouts  93.6 us (14%)
  blocking collectives  32.5 us (5%)
  other arithmetic  24.9 us (4%)
  between operations  19.8 us (3%)
    reduce_scatter x1, waiting for transfers between devices, side_by_side_2(): lax.psum_scatter(both, axis, scatter_dimension=dim, tiled=True)  115 us
    all_gather x2, waiting for transfers between devices, side_by_side(): filled = lax.all_gather(both, axis, axis=dim, tiled=True)  104 us
    dot_general x64, matrix products, add_tile(): jnp.einsum('qhgd,khd->hgqk', query_heads, key_heads, preferred_element_ty...  62.3 us
    dot_general x64, matrix products, add_tile(): jnp.einsum('hgqk,qhgd->khd', prob_half, grad_heads, preferred_element_typ...  51.1 us
    dot_general x64, matrix products, add_tile(): jnp.einsum('qhgd,khd->hgqk', grad_heads, value_heads, preferred_element_t...  48.3 us
    dot_general x64, matrix products, add_tile(): jnp.einsum('hgqk,qhgd->khd', grad_half, query_heads, preferred_element_ty...  43.4 us
    all_gather x1, blocking collectives, side_by_side(): filled = lax.all_gather(both, axis, axis=dim, tiled=True)  32.5 us
    dot_general x64, matrix products, add_tile(): jnp.einsum('hgqk,khd->qhgd', grad_half, key_heads, preferred_element_type...  32.1 us
  transfers between devices with their start and end apart: 5, of which 5 were waited for; matrix products, arithmetic and copies ran while one was open for 11% of the time, Pallas kernels for 0%

commit v1 on v0

v1 whole, which is shorter than its diff:
```python
import math

import jax
import jax.numpy as jnp
from jax import lax
from jax.experimental import pallas as pl
from jax.experimental.pallas import tpu as pltpu
from jax.sharding import PartitionSpec as P

HEAD_DIM = 128
HEADS = 4
BLOCK = 2048
CHUNK = 128
WAYS = 4
STRIP = CHUNK // WAYS
REACH = 5
KSPAN = 1024
KROWS = KSPAN // WAYS
QROWS = 512
SCALE = HEAD_DIM**-0.5
LOG2E = math.log2(math.e)
EXTRA = 16
OFF_DO = CHUNK
OFF_EXTRA = 2 * CHUNK
OFF_K = OFF_EXTRA + EXTRA
OFF_V = OFF_K + STRIP
PACKED = OFF_V + STRIP
F32 = jnp.float32
BF16 = jnp.bfloat16
VMEM = pl.BlockSpec(memory_space=pltpu.VMEM)
SMEM = pl.BlockSpec(memory_space=pltpu.SMEM)


def pieces(x):
    high = x.astype(BF16)
    rest = x - high.astype(F32)
    middle = rest.astype(BF16)
    low = (rest - middle.astype(F32)).astype(BF16)
    return [high, middle, low]


def pack_kernel(q_ref, k_ref, v_ref, o_ref, g_ref, n_ref, out_ref):
    rows = lax.broadcasted_iota(jnp.int32, (CHUNK, CHUNK), 0)
    cols = lax.broadcasted_iota(jnp.int32, (CHUNK, CHUNK), 1)
    eye = (rows == cols).astype(F32)
    norms = lax.dot_general(
        n_ref[...], eye, (((0,), (0,)), ((), ())),
        precision=lax.Precision.HIGHEST, preferred_element_type=F32,
    ) * LOG2E
    ones = jnp.ones((8, HEAD_DIM), F32)
    for h in range(HEADS):
        at = slice(h * HEAD_DIM, (h + 1) * HEAD_DIM)
        q, g = q_ref[:, at], g_ref[:, at]
        delta = lax.dot_general(
            ones, g.astype(F32) * o_ref[:, at].astype(F32), (((1,), (1,)), ((), ())),
            precision=lax.Precision.HIGHEST, preferred_element_type=F32,
        )[:1]
        extra = jnp.concatenate(
            [p.astype(F32) for p in pieces(norms[h : h + 1]) + pieces(delta)]
            + [jnp.zeros((EXTRA - 6, CHUNK), F32)], axis=0
        ).astype(BF16)
        for d in range(WAYS):
            t = h * WAYS + d
            out_ref[t, 0:CHUNK] = q
            out_ref[t, OFF_DO : OFF_DO + CHUNK] = g
            out_ref[t, OFF_EXTRA : OFF_EXTRA + EXTRA] = extra
            out_ref[t, OFF_K : OFF_K + STRIP] = k_ref[d * STRIP : (d + 1) * STRIP, at]
            out_ref[t, OFF_V : OFF_V + STRIP] = v_ref[d * STRIP : (d + 1) * STRIP, at]


def spread_kernel(in_ref, out_ref):
    count = out_ref.shape[0]
    for b in range(count):
        for back in range(REACH):
            out_ref[b, back] = in_ref[max(b - back, 0), OFF_K:PACKED]


def tiles_kernel(place_ref, lengths_ref, in_ref, kv_ref, dq_ref, dkv_ref, dk_acc, dv_acc, dq_acc):
    block = place_ref[0]
    strip = place_ref[1]
    ends = []
    total = jnp.int32(0)
    for e in range(lengths_ref.shape[0]):
        total = total + lengths_ref[e]
        ends.append(total)
    base = (block - (REACH - 1)) * BLOCK
    dk_acc[...] = jnp.zeros_like(dk_acc)
    dv_acc[...] = jnp.zeros_like(dv_acc)
    m_tile = QROWS // CHUNK
    j_tile = KROWS // STRIP
    per_block = BLOCK // KSPAN
    k_iota = lax.broadcasted_iota(jnp.int32, (KROWS, 1), 0)
    k_iota = (k_iota // STRIP) * CHUNK + k_iota % STRIP + strip * STRIP

    def query_tile(t, carry):
        first = block * BLOCK + t * QROWS
        doc_first = jnp.int32(0)
        q_pos = first + lax.broadcasted_iota(jnp.int32, (1, QROWS), 1)
        q_doc = jnp.zeros((1, QROWS), jnp.int32)
        for end in ends:
            doc_first = jnp.where(end <= first, end, doc_first)
            q_doc = jnp.where(end <= q_pos, end, q_doc)
        low = (doc_first - base) // KSPAN
        high = (first + QROWS - 1 - base) // KSPAN
        q = in_ref[pl.ds(t * m_tile, m_tile), 0:CHUNK].reshape(QROWS, HEAD_DIM)
        g = in_ref[pl.ds(t * m_tile, m_tile), OFF_DO : OFF_DO + CHUNK].reshape(QROWS, HEAD_DIM)
        extra = in_ref[pl.ds(t * m_tile, m_tile), OFF_EXTRA : OFF_EXTRA + EXTRA].astype(F32)

        def row(at):
            parts = [
                extra[m, at : at + 1] + extra[m, at + 1 : at + 2] + extra[m, at + 2 : at + 3]
                for m in range(m_tile)
            ]
            return jnp.concatenate(parts, axis=1)

        norm, delta = row(0), row(3)
        dq_acc[...] = jnp.zeros_like(dq_acc)

        def key_tile(kt, carry):
            js = pl.ds((kt % per_block) * j_tile, j_tile)
            back = REACH - 1 - kt // per_block
            k = kv_ref[js, back, 0:STRIP].reshape(KROWS, HEAD_DIM)
            v = kv_ref[js, back, STRIP : 2 * STRIP].reshape(KROWS, HEAD_DIM)
            k_pos = k_iota + (base + kt * KSPAN)
            across = (((1,), (1,)), ((), ()))
            s = lax.dot_general(k, q, across, preferred_element_type=F32)
            p = jnp.exp2(s * (SCALE * LOG2E) - norm)
            p = jnp.where((k_pos <= q_pos) & (k_pos >= q_doc), p, 0.0)
            dp = lax.dot_general(v, g, across, preferred_element_type=F32)
            ds = (p * (dp - delta)).astype(BF16)
            p = p.astype(BF16)
            dv_acc[kt] += jnp.dot(p, g, preferred_element_type=F32)
            dk_acc[kt] += jnp.dot(ds, q, preferred_element_type=F32)
            dq_acc[...] += lax.dot_general(
                ds, k, (((0,), (0,)), ((), ())), preferred_element_type=F32
            )
            return carry

        lax.fori_loop(low, high + 1, key_tile, 0)
        dq_ref[pl.ds(t * m_tile, m_tile)] = (
            (dq_acc[...] * SCALE).astype(BF16).reshape(m_tile, CHUNK, HEAD_DIM)
        )
        return carry

    lax.fori_loop(0, BLOCK // QROWS, query_tile, 0)
    for kt in range(REACH * per_block):
        js = slice((kt % per_block) * j_tile, (kt % per_block + 1) * j_tile)
        back = REACH - 1 - kt // per_block
        dkv_ref[js, back, 0:STRIP] = (dk_acc[kt] * SCALE).astype(BF16).reshape(j_tile, STRIP, HEAD_DIM)
        dkv_ref[js, back, STRIP : 2 * STRIP] = dv_acc[kt].astype(BF16).reshape(j_tile, STRIP, HEAD_DIM)


def collect_kernel(dq_ref, dkv_ref, out_ref):
    count = out_ref.shape[0]
    for b in range(count):
        out_ref[b, 0:CHUNK] = dq_ref[b]
        total = dkv_ref[b, 0].astype(F32)
        for back in range(1, REACH):
            if b + back < count:
                total = total + dkv_ref[b + back, back].astype(F32)
        out_ref[b, CHUNK : CHUNK + 2 * STRIP] = total.astype(BF16)


def unpack_kernel(in_ref, dq_ref, dk_ref, dv_ref):
    for h in range(HEADS):
        at = slice(h * HEAD_DIM, (h + 1) * HEAD_DIM)
        total = in_ref[h * WAYS, 0:CHUNK].astype(F32)
        for d in range(1, WAYS):
            total = total + in_ref[h * WAYS + d, 0:CHUNK].astype(F32)
        dq_ref[:, at] = total.astype(BF16)
        for d in range(WAYS):
            rows = slice(d * STRIP, (d + 1) * STRIP)
            dk_ref[rows, at] = in_ref[h * WAYS + d, CHUNK : CHUNK + STRIP]
            dv_ref[rows, at] = in_ref[h * WAYS + d, CHUNK + STRIP : CHUNK + 2 * STRIP]


def shape(*dims, dtype=BF16):
    return jax.ShapeDtypeStruct(dims, dtype)


def per_device(query_states, key_states, value_states, saved_output, output_grad, normalizer, doc_lengths):
    blocks = lax.axis_size("qrow")
    ways = lax.axis_size("kcol")
    place = jnp.stack([lax.axis_index("qrow"), lax.axis_index("kcol") % WAYS]).astype(jnp.int32)
    packed = pl.pallas_call(
        pack_kernel,
        in_specs=[VMEM] * 6,
        out_specs=VMEM,
        out_shape=shape(ways, PACKED, HEAD_DIM),
    )(query_states, key_states, value_states, saved_output, output_grad, normalizer)
    mine = lax.all_to_all(packed, "kcol", 0, 0)
    spread = pl.pallas_call(
        spread_kernel,
        in_specs=[VMEM],
        out_specs=VMEM,
        out_shape=shape(blocks, REACH, 2 * STRIP, HEAD_DIM),
    )(mine)
    keys = lax.all_to_all(spread, "qrow", 0, 0)
    tiles = REACH * BLOCK // KSPAN
    dq_part, dkv_part = pl.pallas_call(
        tiles_kernel,
        in_specs=[SMEM, SMEM, VMEM, VMEM],
        out_specs=[VMEM, VMEM],
        out_shape=[shape(ways, CHUNK, HEAD_DIM), shape(blocks, REACH, 2 * STRIP, HEAD_DIM)],
        scratch_shapes=[
            pltpu.VMEM((tiles, KROWS, HEAD_DIM), F32),
            pltpu.VMEM((tiles, KROWS, HEAD_DIM), F32),
            pltpu.VMEM((QROWS, HEAD_DIM), F32),
        ],
        compiler_params=pltpu.CompilerParams(vmem_limit_bytes=40 * 1024 * 1024),
    )(place, doc_lengths, mine, keys)
    dkv = lax.all_to_all(dkv_part, "qrow", 0, 0)
    sums = pl.pallas_call(
        collect_kernel,
        in_specs=[VMEM, VMEM],
        out_specs=VMEM,
        out_shape=shape(ways, CHUNK + 2 * STRIP, HEAD_DIM),
    )(dq_part, dkv)
    back = lax.all_to_all(sums, "kcol", 0, 0)
    width = HEADS * HEAD_DIM
    return tuple(
        pl.pallas_call(
            unpack_kernel,
            in_specs=[VMEM],
            out_specs=[VMEM] * 3,
            out_shape=[shape(CHUNK, width)] * 3,
        )(back)
    )


def solution(mesh):
    rows = P(("qrow", "kcol"), None)
    keys = P(("kcol", "qrow"), None)
    return jax.shard_map(
        per_device,
        mesh=mesh,
        in_specs=(rows, keys, keys, rows, rows, rows, P()),
        out_specs=(rows, keys, keys),
        check_vma=False,
    )
```

time: 659 us -> 152 us (0.23)
  matrix products: 237 us -> 0 us
  waiting for transfers between devices: 243 us -> 20.7 us
  local copies, waits for them, and re-layouts: 93.6 us -> 1.43 us
  blocking collectives: 32.5 us -> 106 us
  other arithmetic: 24.9 us -> 0.08 us
  between operations: 19.8 us -> 0.67 us
  Pallas kernels: 0 us -> 14.8 us
    dot_general x320 -> x0, matrix products: 237 us -> none  [the longest x64 62.3 us: add_tile(): jnp.einsum('qhgd,khd->hgqk', query_heads, key_heads, preferred_element_ty...]
    reduce_scatter x3 -> x0, waiting for transfers between devices: 139 us -> none  [the longest x1 115 us: side_by_side_2(): lax.psum_scatter(both, axis, scatter_dimension=dim, tiled=True)]
    all_to_all x0 -> x3, blocking collectives: none -> 106 us  [the longest x1 43.3 us: per_device(): mine = lax.all_to_all(packed, 'kcol', 0, 0)]
    all_gather x2 -> x0, waiting for transfers between devices: 104 us -> none  [side_by_side(): filled = lax.all_gather(both, axis, axis=dim, tiled=True)]
    add x24 -> x0, local copies, waits for them, and re-layouts: 49.3 us -> none  [the longest x8 16.5 us: add_tile(): key_acc + key_add.reshape(key_count, KV_HEADS * HEAD_DIM)]
    all_gather x1 -> x0, blocking collectives: 32.5 us -> none  [side_by_side(): filled = lax.all_gather(both, axis, axis=dim, tiled=True)]
    unnamed x707 -> x7, local copies, waits for them, and re-layouts: 30.7 us -> 1.43 us
    all_to_all x0 -> x1, waiting for transfers between devices: none -> 20.7 us  [per_device(): keys = lax.all_to_all(spread, 'qrow', 0, 0)]
  transfers between devices with their start and end apart: 5 -> 1, of which waited for: 5 -> 1; matrix products, arithmetic and copies ran while one was open for 11% -> 0% of each run, Pallas kernels for 0% -> 0%
where the time goes in v1:
time: 152 us; the launch traced here: 150 us
  blocking collectives  106 us (70%)
  waiting for transfers between devices  20.7 us (14%)
  Pallas kernels  14.8 us (10%)
  starting transfers between devices  6.27 us (4%)
    all_to_all x1, blocking collectives, per_device(): mine = lax.all_to_all(packed, 'kcol', 0, 0)  43.3 us
    all_to_all x1, blocking collectives, per_device(): dkv = lax.all_to_all(dkv_part, 'qrow', 0, 0)  36.2 us
    all_to_all x1, blocking collectives, per_device(): back = lax.all_to_all(sums, 'kcol', 0, 0)  26.8 us
    all_to_all x1, waiting for transfers between devices, per_device(): keys = lax.all_to_all(spread, 'qrow', 0, 0)  20.7 us
    all_to_all x1, starting transfers between devices, per_device(): keys = lax.all_to_all(spread, 'qrow', 0, 0)  6.27 us
    pallas_call x1, Pallas kernels, per_device(): pl.pallas_call(tiles_kernel, in_specs=[SMEM, SMEM, VMEM, VMEM], out_specs...  4.89 us
  transfers between devices with their start and end apart: 1, of which 1 were waited for; matrix products, arithmetic and copies ran while one was open for 0% of the time, Pallas kernels for 0%

profile of v1, /device:TPU:40, one launch (start us, length us, event | category | flops | bytes accessed | tf_op | source)
XLA Modules:
  0.0 150.1 jit_solution(12281778322824681053)
XLA Ops:
  0.6 1.4 copy.10.n_ref
  2.0 2.9 %shard_map.94 = bf16[16,336,128]{2,1,0:T(8,128)(2,1)} custom-call(bf16[128,512]{1,0:T(8,128)(2,1)} %q_ref.1, bf16[128,512]{1,0:T(8,128)(2,1)} %k_ref.1, bf16[128,512]{1,0:T(8,128)(2,1)} %v_ref.1, bf16[128,512]{1,0:T(8,128)(2,1)} %o_ref.1, bf16[128,512]{1,0:T(8,128)(2,1)} %g_ref.1, f32[128,4]{1,0:T(8,128)} %copy.10.n_ref), custom_call_target="tpu_custom_call" | custom-call | tf_op jit(solution)/shard_map/pallas_call | solution.py:185
  4.9 43.3 %all_to_all.20.in_ref = bf16[16,336,128]{2,1,0:T(8,128)(2,1)} all-to-all(bf16[16,336,128]{2,1,0:T(8,128)(2,1)} %shard_map.94), channel_id=1, replica_groups=mesh['qrow'=16,'kcol'=16] {'kcol'}, dimensions={0} | all-to-all | bytes 2752512 | tf_op jit(solution)/shard_map/all_to_all | solution.py:191
  48.2 2.6 %shard_map.95 = bf16[16,5,64,128]{3,2,1,0:T(8,128)(2,1)} custom-call(bf16[16,336,128]{2,1,0:T(8,128)(2,1)} %all_to_all.20.in_ref), custom_call_target="tpu_custom_call" | custom-call | tf_op jit(solution)/shard_map/pallas_call | solution.py:192
  50.8 0.0 copy-start
  50.8 0.0 copy-start.2
  50.8 6.3 %all-to-all-start.1 = ((bf16[16,5,64,128]{3,2,1,0:T(8,128)(2,1)}), bf16[16,5,64,128]{3,2,1,0:T(8,128)(2,1)S(1)}, u32[]{:S(2)}, u32[]{:S(2)}) async-start(bf16[16,5,64,128]{3,2,1,0:T(8,128)(2,1)} %shard_map.95), calls=%async_computation.1 | async-start | bytes 2621440 | tf_op jit(solution)/shard_map/all_to_all | solution.py:198
  57.0 0.1 pad_add_fusion.place_ref
  57.1 20.7 %all-to-all-done.1.kv_ref = bf16[16,5,64,128]{3,2,1,0:T(8,128)(2,1)S(1)} async-done(((bf16[16,5,64,128]{3,2,1,0:T(8,128)(2,1)}), bf16[16,5,64,128]{3,2,1,0:T(8,128)(2,1)S(1)}, u32[]{:S(2)}, u32[]{:S(2)}) %all-to-all-start.1) | async-done | bytes 1310752 | tf_op jit(solution)/shard_map/all_to_all | solution.py:198
  77.8 0.0 copy-done
  77.8 0.0 copy-done.2
  77.8 4.9 %shard_map.96 = (bf16[16,128,128]{2,1,0:T(8,128)(2,1)S(1)}, bf16[16,5,64,128]{3,2,1,0:T(8,128)(2,1)S(1)}) custom-call(s32[2]{0:T(128)S(1)} %pad_add_fusion.place_ref, s32[8]{0:T(128)S(1)} %copy-done.2, bf16[16,336,128]{2,1,0:T(8,128)(2,1)S(1)} %copy-done, bf16[16,5,64,128]{3,2,1,0:T(8,128)(2,1)S(1)} %all-to-all-done.1.kv_ref), custom_call_target="tpu_custom_call" | custom-call | tf_op jit(solution)/shard_map/pallas_call | solution.py:200
  82.7 0.0 copy-start.1
  82.7 36.2 %all_to_all.21.dkv_ref = bf16[16,5,64,128]{3,2,1,0:T(8,128)(2,1)} all-to-all(bf16[16,5,64,128]{3,2,1,0:T(8,128)(2,1)S(1)} %get-tuple-element.6), channel_id=1, replica_groups=mesh['qrow'=16,'kcol'=16] {'qrow'}, dimensions={0} | all-to-all | bytes 2621440 | tf_op jit(solution)/shard_map/all_to_all | solution.py:212
  118.9 0.0 copy-done.1
  118.9 2.5 %shard_map.97 = bf16[16,192,128]{2,1,0:T(8,128)(2,1)} custom-call(bf16[16,128,128]{2,1,0:T(8,128)(2,1)} %copy-done.1, bf16[16,5,64,128]{3,2,1,0:T(8,128)(2,1)} %all_to_all.21.dkv_ref), custom_call_target="tpu_custom_call" | custom-call | tf_op jit(solution)/shard_map/pallas_call | solution.py:213
  121.4 26.8 %all_to_all.22.in_ref = bf16[16,192,128]{2,1,0:T(8,128)(2,1)} all-to-all(bf16[16,192,128]{2,1,0:T(8,128)(2,1)} %shard_map.97), channel_id=1, replica_groups=mesh['qrow'=16,'kcol'=16] {'kcol'}, dimensions={0} | all-to-all | bytes 1572864 | tf_op jit(solution)/shard_map/all_to_all | solution.py:219
  148.2 1.9 %shard_map.98 = (bf16[128,512]{1,0:T(8,128)(2,1)}, bf16[128,512]{1,0:T(8,128)(2,1)}, bf16[128,512]{1,0:T(8,128)(2,1)}) custom-call(bf16[16,192,128]{2,1,0:T(8,128)(2,1)} %all_to_all.22.in_ref), custom_call_target="tpu_custom_call" | custom-call | tf_op jit(solution)/shard_map/pallas_call | solution.py:222
Async XLA Ops:
  50.8 27.1 %copy-start = (bf16[16,336,128]{2,1,0:T(8,128)(2,1)S(1)}, bf16[16,336,128]{2,1,0:T(8,128)(2,1)}, u32[]{:S(2)}) copy-start(bf16[16,336,128]{2,1,0:T(8,128)(2,1)} %all_to_all.20.in_ref) | copy-start | bytes 4128772
  50.8 27.1 %copy-start.2 = (s32[8]{0:T(128)S(1)}, s32[8]{0:T(128)}, u32[]{:S(2)}) copy-start(s32[8]{0:T(128)} %lengths_ref.1) | copy-start | bytes 100
  50.8 27.1 %all-to-all-start.1 = ((bf16[16,5,64,128]{3,2,1,0:T(8,128)(2,1)}), bf16[16,5,64,128]{3,2,1,0:T(8,128)(2,1)S(1)}, u32[]{:S(2)}, u32[]{:S(2)}) async-start(bf16[16,5,64,128]{3,2,1,0:T(8,128)(2,1)} %shard_map.95), calls=%async_computation.1 | async-start | bytes 2621440 | tf_op jit(solution)/shard_map/all_to_all | solution.py:198
  82.7 36.2 %copy-start.1 = (bf16[16,128,128]{2,1,0:T(8,128)(2,1)}, bf16[16,128,128]{2,1,0:T(8,128)(2,1)S(1)}, u32[]{:S(2)}) copy-start(bf16[16,128,128]{2,1,0:T(8,128)(2,1)S(1)} %get-tuple-element.5.dq_ref) | copy-start | bytes 1572868

commit v2 on v1

v2 whole, which is shorter than its diff:
```python
import math

import jax
import jax.numpy as jnp
from jax import lax
from jax.experimental import pallas as pl
from jax.experimental.pallas import tpu as pltpu
from jax.sharding import Mesh
from jax.sharding import PartitionSpec as P

HEAD_DIM = 128
HEADS = 4
BLOCK = 2048
CHUNK = 128
WAYS = 4
STRIP = CHUNK // WAYS
REACH = 5
KSPAN = 1024
KROWS = KSPAN // WAYS
QROWS = 1024
SCALE = HEAD_DIM**-0.5
LOG2E = math.log2(math.e)
EXTRA = 16
OFF_DO = STRIP
OFF_K = 2 * STRIP
OFF_V = 3 * STRIP
OFF_EXTRA = 4 * STRIP
PACKED = OFF_EXTRA + EXTRA
KCOL = ("kcol_h", "kcol_s")
STRIPS = "kcol_s"
F32 = jnp.float32
BF16 = jnp.bfloat16
VMEM = pl.BlockSpec(memory_space=pltpu.VMEM)
SMEM = pl.BlockSpec(memory_space=pltpu.SMEM)


def pieces(x):
    high = x.astype(BF16)
    rest = x - high.astype(F32)
    middle = rest.astype(BF16)
    low = (rest - middle.astype(F32)).astype(BF16)
    return [high, middle, low]


def head_and_strip(t):
    return t // WAYS, t % WAYS


def pack_kernel(q_ref, k_ref, v_ref, o_ref, g_ref, n_ref, out_ref):
    norms = n_ref[...] * LOG2E
    ones = jnp.ones((8, HEAD_DIM), F32)
    extras = []
    for h in range(HEADS):
        at = slice(h * HEAD_DIM, (h + 1) * HEAD_DIM)
        delta = lax.dot_general(
            ones, g_ref[:, at].astype(F32) * o_ref[:, at].astype(F32), (((1,), (1,)), ((), ())),
            precision=lax.Precision.HIGHEST, preferred_element_type=F32,
        )[:1]
        extras.append(
            jnp.concatenate(
                [p.astype(F32) for p in pieces(norms[h : h + 1]) + pieces(delta)]
                + [jnp.zeros((EXTRA - 6, CHUNK), F32)], axis=0
            ).astype(BF16)
        )
    for t in range(out_ref.shape[0]):
        h, d = head_and_strip(t)
        at = slice(h * HEAD_DIM, (h + 1) * HEAD_DIM)
        rows = slice(d * STRIP, (d + 1) * STRIP)
        out_ref[t, 0:STRIP] = q_ref[rows, at]
        out_ref[t, OFF_DO : OFF_DO + STRIP] = g_ref[rows, at]
        out_ref[t, OFF_K : OFF_K + STRIP] = k_ref[rows, at]
        out_ref[t, OFF_V : OFF_V + STRIP] = v_ref[rows, at]
        out_ref[t, OFF_EXTRA:PACKED] = extras[h]


def spread_kernel(in_ref, out_ref, qg_ref):
    count = out_ref.shape[0]
    qg_ref[...] = in_ref[:, 0 : 2 * STRIP]
    for b in range(count):
        for back in range(REACH):
            out_ref[b, back] = in_ref[max(b - back, 0), OFF_K : OFF_K + 2 * STRIP]


def tiles_kernel(
    place_ref, lengths_ref, in_ref, qg0, qg1, qg2, qg3, kv_ref,
    dq0, dq1, dq2, dq3, dkv_ref, dk_acc, dv_acc, dq_acc, q_all, g_all, dq_all,
):
    block = place_ref[0]
    strip = place_ref[1]
    ends = []
    total = jnp.int32(0)
    for e in range(lengths_ref.shape[0]):
        total = total + lengths_ref[e]
        ends.append(total)
    base = (block - (REACH - 1)) * BLOCK
    for s, ref in enumerate((qg0, qg1, qg2, qg3)):
        q_all[:, strip ^ s] = ref[:, 0:STRIP]
        g_all[:, strip ^ s] = ref[:, STRIP : 2 * STRIP]
    dk_acc[...] = jnp.zeros_like(dk_acc)
    dv_acc[...] = jnp.zeros_like(dv_acc)
    m_tile = QROWS // CHUNK
    j_tile = KROWS // STRIP
    per_block = BLOCK // KSPAN
    k_iota = lax.broadcasted_iota(jnp.int32, (KROWS, 1), 0)
    k_iota = (k_iota // STRIP) * CHUNK + k_iota % STRIP + strip * STRIP

    def query_tile(t, carry):
        first = block * BLOCK + t * QROWS
        last = first + QROWS - 1
        doc_first = jnp.int32(0)
        doc_last = jnp.int32(0)
        q_pos = first + lax.broadcasted_iota(jnp.int32, (1, QROWS), 1)
        q_doc = jnp.zeros((1, QROWS), jnp.int32)
        for end in ends:
            doc_first = jnp.where(end <= first, end, doc_first)
            doc_last = jnp.where(end <= last, end, doc_last)
            q_doc = jnp.where(end <= q_pos, end, q_doc)
        low = (doc_first - base) // KSPAN
        high = (last - base) // KSPAN
        q = q_all[pl.ds(t * m_tile, m_tile)].reshape(QROWS, HEAD_DIM)
        g = g_all[pl.ds(t * m_tile, m_tile)].reshape(QROWS, HEAD_DIM)
        extra = in_ref[pl.ds(t * m_tile, m_tile), OFF_EXTRA:PACKED].astype(F32)

        def row(at):
            parts = [
                extra[m, at : at + 1] + extra[m, at + 1 : at + 2] + extra[m, at + 2 : at + 3]
                for m in range(m_tile)
            ]
            return jnp.concatenate(parts, axis=1)

        norm, delta = row(0), row(3)
        dq_acc[...] = jnp.zeros_like(dq_acc)

        def one_tile(kt, masked):
            js = pl.ds((kt % per_block) * j_tile, j_tile)
            back = REACH - 1 - kt // per_block
            k = kv_ref[js, back, 0:STRIP].reshape(KROWS, HEAD_DIM)
            v = kv_ref[js, back, STRIP : 2 * STRIP].reshape(KROWS, HEAD_DIM)
            across = (((1,), (1,)), ((), ()))
            s = lax.dot_general(k, q, across, preferred_element_type=F32)
            p = jnp.exp2(s * (SCALE * LOG2E) - norm)
            if masked:
                k_pos = k_iota + (base + kt * KSPAN)
                p = jnp.where((k_pos <= q_pos) & (k_pos >= q_doc), p, 0.0)
            dp = lax.dot_general(v, g, across, preferred_element_type=F32)
            ds = (p * (dp - delta)).astype(BF16)
            p = p.astype(BF16)
            dv_acc[kt] += jnp.dot(p, g, preferred_element_type=F32)
            dk_acc[kt] += jnp.dot(ds, q, preferred_element_type=F32)
            dq_acc[...] += lax.dot_general(
                k, ds, (((0,), (0,)), ((), ())), preferred_element_type=F32
            )

        def key_tile(kt, carry):
            start = base + kt * KSPAN
            whole = (start + KSPAN - 1 <= first) & (start >= doc_last)

            @pl.when(whole)
            def _():
                one_tile(kt, False)

            @pl.when(jnp.logical_not(whole))
            def _():
                one_tile(kt, True)

            return carry

        lax.fori_loop(low, high + 1, key_tile, 0)
        dq_all[pl.ds(t * m_tile, m_tile)] = (
            (dq_acc[...].T * SCALE).astype(BF16).reshape(m_tile, WAYS, STRIP, HEAD_DIM)
        )
        return carry

    lax.fori_loop(0, BLOCK // QROWS, query_tile, 0)
    for s, ref in enumerate((dq0, dq1, dq2, dq3)):
        ref[...] = dq_all[:, strip ^ s]
    for kt in range(REACH * per_block):
        js = slice((kt % per_block) * j_tile, (kt % per_block + 1) * j_tile)
        back = REACH - 1 - kt // per_block
        dkv_ref[js, back, 0:STRIP] = (dk_acc[kt] * SCALE).astype(BF16).reshape(j_tile, STRIP, HEAD_DIM)
        dkv_ref[js, back, STRIP : 2 * STRIP] = dv_acc[kt].astype(BF16).reshape(j_tile, STRIP, HEAD_DIM)


def collect_kernel(dq0, dq1, dq2, dq3, dkv_ref, out_ref):
    count = out_ref.shape[0]
    dq = dq0[...].astype(F32)
    for ref in (dq1, dq2, dq3):
        dq = dq + ref[...].astype(F32)
    out_ref[:, 0:STRIP] = dq.astype(BF16)
    for b in range(count):
        total = dkv_ref[b, 0].astype(F32)
        for back in range(1, REACH):
            if b + back < count:
                total = total + dkv_ref[b + back, back].astype(F32)
        out_ref[b, STRIP : 3 * STRIP] = total.astype(BF16)


def unpack_kernel(in_ref, dq_ref, dk_ref, dv_ref):
    for t in range(in_ref.shape[0]):
        h, d = head_and_strip(t)
        at = slice(h * HEAD_DIM, (h + 1) * HEAD_DIM)
        rows = slice(d * STRIP, (d + 1) * STRIP)
        dq_ref[rows, at] = in_ref[t, 0:STRIP]
        dk_ref[rows, at] = in_ref[t, STRIP : 2 * STRIP]
        dv_ref[rows, at] = in_ref[t, 2 * STRIP : 3 * STRIP]


def shape(*dims, dtype=BF16):
    return jax.ShapeDtypeStruct(dims, dtype)


def from_partner(x, s):
    return lax.ppermute(x, STRIPS, [(d, d ^ s) for d in range(WAYS)])


def call_tiles(place, doc_lengths, mine, qg, *rest):
    keys = rest[-1]
    ways, blocks = mine.shape[0], keys.shape[0]
    tiles = REACH * BLOCK // KSPAN
    return pl.pallas_call(
        tiles_kernel,
        in_specs=[SMEM, SMEM] + [VMEM] * 6,
        out_specs=[VMEM] * 5,
        out_shape=[shape(ways, STRIP, HEAD_DIM)] * 4 + [shape(blocks, REACH, 2 * STRIP, HEAD_DIM)],
        scratch_shapes=[
            pltpu.VMEM((tiles, KROWS, HEAD_DIM), F32),
            pltpu.VMEM((tiles, KROWS, HEAD_DIM), F32),
            pltpu.VMEM((HEAD_DIM, QROWS), F32),
        ] + [pltpu.VMEM((ways, WAYS, STRIP, HEAD_DIM), BF16)] * 3,
        compiler_params=pltpu.CompilerParams(vmem_limit_bytes=40 * 1024 * 1024),
    )(place, doc_lengths, mine, qg, *rest)


def per_device(query_states, key_states, value_states, saved_output, output_grad, normalizer, doc_lengths):
    blocks = lax.axis_size("qrow")
    ways = lax.axis_size(KCOL)
    place = jnp.stack([lax.axis_index("qrow"), lax.axis_index(STRIPS)]).astype(jnp.int32)
    packed = pl.pallas_call(
        pack_kernel,
        in_specs=[VMEM] * 6,
        out_specs=VMEM,
        out_shape=shape(ways, PACKED, HEAD_DIM),
    )(query_states, key_states, value_states, saved_output, output_grad, normalizer.T)
    mine = lax.all_to_all(packed, KCOL, 0, 0)
    spread, qg = pl.pallas_call(
        spread_kernel,
        in_specs=[VMEM],
        out_specs=[VMEM] * 2,
        out_shape=[shape(blocks, REACH, 2 * STRIP, HEAD_DIM), shape(ways, 2 * STRIP, HEAD_DIM)],
    )(mine)
    keys = lax.all_to_all(spread, "qrow", 0, 0)
    far = from_partner(qg, 2)
    others = [from_partner(qg, 1), far, from_partner(far, 1)]
    *dq_parts, dkv_part = call_tiles(place, doc_lengths, mine, qg, *others, keys)
    dkv = lax.all_to_all(dkv_part, "qrow", 0, 0)
    dq_parts = [dq_parts[0]] + [from_partner(dq_parts[s], s) for s in range(1, WAYS)]
    sums = pl.pallas_call(
        collect_kernel,
        in_specs=[VMEM] * 5,
        out_specs=VMEM,
        out_shape=shape(ways, 3 * STRIP, HEAD_DIM),
    )(*dq_parts, dkv)
    back = lax.all_to_all(sums, KCOL, 0, 0)
    width = HEADS * HEAD_DIM
    return tuple(
        pl.pallas_call(
            unpack_kernel,
            in_specs=[VMEM],
            out_specs=[VMEM] * 3,
            out_shape=[shape(CHUNK, width)] * 3,
        )(back)
    )


def solution(mesh):
    finer = Mesh(mesh.devices.reshape(mesh.shape["qrow"], HEADS, WAYS), ("qrow",) + KCOL)
    rows = P(("qrow",) + KCOL, None)
    keys = P(KCOL + ("qrow",), None)
    return jax.shard_map(
        per_device,
        mesh=finer,
        in_specs=(rows, keys, keys, rows, rows, rows, P()),
        out_specs=(rows, keys, keys),
        check_vma=False,
    )
```

time: 152 us -> 130 us (0.86); the launches traced: 150 us -> 132 us
  blocking collectives: 106 us -> 46.7 us
  starting transfers between devices: 6.27 us -> 35 us
  waiting for transfers between devices: 20.7 us -> 33.8 us
    all_to_all x3 -> x2, blocking collectives: 106 us -> 46.7 us  [the longest x1 26.9 us: per_device(): mine = lax.all_to_all(packed, KCOL, 0, 0)]
    ppermute x0 -> x6, waiting for transfers between devices: none -> 28.6 us  [from_partner(): return lax.ppermute(x, STRIPS, [(d, d ^ s) for d in range(WAYS)])]
    all_to_all x1, waiting for transfers between devices: 20.7 us -> 0.01 us  [per_device(): keys = lax.all_to_all(spread, 'qrow', 0, 0)]
    all_to_all x0 -> x1, starting transfers between devices: none -> 19.1 us  [per_device(): dkv = lax.all_to_all(dkv_part, 'qrow', 0, 0)]
    ppermute x0 -> x6, starting transfers between devices: none -> 9.65 us  [from_partner(): return lax.ppermute(x, STRIPS, [(d, d ^ s) for d in range(WAYS)])]
    all_to_all x0 -> x1, waiting for transfers between devices: none -> 5.23 us  [per_device(): dkv = lax.all_to_all(dkv_part, 'qrow', 0, 0)]
  transfers between devices with their start and end apart: 1 -> 8, of which waited for: 1 -> 6; matrix products, arithmetic and copies ran while one was open for 0% -> 0% of each run, Pallas kernels for 0% -> 0%
where the time goes in v2:
time: 130 us; the launch traced here: 132 us
  blocking collectives  46.7 us (36%)
  starting transfers between devices  35 us (27%)
  waiting for transfers between devices  33.8 us (26%)
  Pallas kernels  14.4 us (11%)
  local copies, waits for them, and re-layouts  1.75 us (1%)
    ppermute x6, waiting for transfers between devices, from_partner(): return lax.ppermute(x, STRIPS, [(d, d ^ s) for d in range(WAYS)])  28.6 us
    all_to_all x1, blocking collectives, per_device(): mine = lax.all_to_all(packed, KCOL, 0, 0)  26.9 us
    all_to_all x1, blocking collectives, per_device(): back = lax.all_to_all(sums, KCOL, 0, 0)  19.8 us
    all_to_all x1, starting transfers between devices, per_device(): dkv = lax.all_to_all(dkv_part, 'qrow', 0, 0)  19.1 us
    ppermute x6, starting transfers between devices, from_partner(): return lax.ppermute(x, STRIPS, [(d, d ^ s) for d in range(WAYS)])  9.65 us
    all_to_all x1, starting transfers between devices, per_device(): keys = lax.all_to_all(spread, 'qrow', 0, 0)  6.28 us
    all_to_all x1, waiting for transfers between devices, per_device(): dkv = lax.all_to_all(dkv_part, 'qrow', 0, 0)  5.23 us
    pallas_call x1, Pallas kernels, call_tiles(): pl.pallas_call(tiles_kernel, in_specs=[SMEM, SMEM] + [VMEM] * 6, out_spec...  5.19 us
  transfers between devices with their start and end apart: 8, of which 6 were waited for; matrix products, arithmetic and copies ran while one was open for 0% of the time, Pallas kernels for 0%

profile of v2, /device:TPU:40, one launch (start us, length us, event | category | flops | bytes accessed | tf_op | source)
XLA Modules:
  0.0 132.4 jit_solution(9450424188652825293)
XLA Ops:
  0.6 2.5 %shard_map.94 = bf16[16,144,128]{2,1,0:T(8,128)(2,1)} custom-call(bf16[128,512]{1,0:T(8,128)(2,1)} %q_ref.1, bf16[128,512]{1,0:T(8,128)(2,1)} %k_ref.1, bf16[128,512]{1,0:T(8,128)(2,1)} %v_ref.1, bf16[128,512]{1,0:T(8,128)(2,1)} %o_ref.1, bf16[128,512]{1,0:T(8,128)(2,1)} %g_ref.1, f32[4,128]{1,0:T(4,128)} %bitcast.3), custom_call_target="tpu_custom_call" | custom-call | tf_op jit(solution)/shard_map/pallas_call | solution.py:238
  3.2 26.9 %all_to_all.20.in_ref = bf16[16,144,128]{2,1,0:T(8,128)(2,1)} all-to-all(bf16[16,144,128]{2,1,0:T(8,128)(2,1)} %shard_map.94), channel_id=1, replica_groups=mesh['qrow'=16,'kcol_h'=4,'kcol_s'=4] {'kcol_h','kcol_s'}, dimensions={0} | all-to-all | bytes 1179648 | tf_op jit(solution)/shard_map/all_to_all | solution.py:244
  30.1 2.3 %shard_map.95 = (bf16[16,5,64,128]{3,2,1,0:T(8,128)(2,1)}, bf16[16,64,128]{2,1,0:T(8,128)(2,1)}) custom-call(bf16[16,144,128]{2,1,0:T(8,128)(2,1)} %all_to_all.20.in_ref), custom_call_target="tpu_custom_call" | custom-call | tf_op jit(solution)/shard_map/pallas_call | solution.py:245
  32.4 6.3 %all-to-all-start.1 = ((bf16[16,5,64,128]{3,2,1,0:T(8,128)(2,1)}), bf16[16,5,64,128]{3,2,1,0:T(8,128)(2,1)S(1)}, u32[]{:S(2)}, u32[]{:S(2)}) async-start(bf16[16,5,64,128]{3,2,1,0:T(8,128)(2,1)} %get-tuple-element.11), calls=%async_computation.1 | async-start | bytes 2621440 | tf_op jit(solution)/shard_map/all_to_all | solution.py:251
  38.7 0.0 copy-done.1
  38.7 0.7 collective-permute-start.1
  39.5 1.4 %collective-permute-start = (bf16[16,64,128]{2,1,0:T(8,128)(2,1)S(1)}, bf16[16,64,128]{2,1,0:T(8,128)(2,1)S(1)}, u32[]{:S(2)}, u32[]{:S(2)}) collective-permute-start(bf16[16,64,128]{2,1,0:T(8,128)(2,1)S(1)} %copy-done.1), channel_id=1, source_target_pairs={{0,1},{1,0},{2,3},{3,2},{4,5},{5,4},{6,7},{7,6},{8,9},{9,8},{10,11... | collective-permute-start | bytes 786440 | tf_op jit(solution)/shard_map/ppermute | solution.py:213
  40.9 10.4 %collective-permute-done.1.qg2 = bf16[16,64,128]{2,1,0:T(8,128)(2,1)S(1)} collective-permute-done((bf16[16,64,128]{2,1,0:T(8,128)(2,1)S(1)}, bf16[16,64,128]{2,1,0:T(8,128)(2,1)S(1)}, u32[]{:S(2)}, u32[]{:S(2)}) %collective-permute-start.1) | collective-permute-done | bytes 262176 | tf_op jit(solution)/shard_map/ppermute | solution.py:213
  51.3 3.9 %collective-permute-start.2 = (bf16[16,64,128]{2,1,0:T(8,128)(2,1)S(1)}, bf16[16,64,128]{2,1,0:T(8,128)(2,1)S(1)}, u32[]{:S(2)}, u32[]{:S(2)}) collective-permute-start(bf16[16,64,128]{2,1,0:T(8,128)(2,1)S(1)} %collective-permute-done.1.qg2), channel_id=1, source_target_pairs={{0,1},{1,0},{2,3},{3,2},{4,5},{5,4},{6,7},{7,6},{8,9},{9,8},{10,11... | collective-permute-start | bytes 786440 | tf_op jit(solution)/shard_map/ppermute | solution.py:213
  55.2 0.1 pad_add_fusion.place_ref
  55.3 0.0 collective-permute-done.qg1
  55.3 6.2 %collective-permute-done.2.qg3 = bf16[16,64,128]{2,1,0:T(8,128)(2,1)S(1)} collective-permute-done((bf16[16,64,128]{2,1,0:T(8,128)(2,1)S(1)}, bf16[16,64,128]{2,1,0:T(8,128)(2,1)S(1)}, u32[]{:S(2)}, u32[]{:S(2)}) %collective-permute-start.2) | collective-permute-done | bytes 262176 | tf_op jit(solution)/shard_map/ppermute | solution.py:213
  61.5 0.0 all-to-all-done.1.kv_ref
  61.5 0.0 copy-done
  61.5 0.0 copy-done.3
  61.5 5.2 %shard_map.96 = (bf16[16,32,128]{2,1,0:T(8,128)(2,1)S(1)}, bf16[16,32,128]{2,1,0:T(8,128)(2,1)S(1)}, bf16[16,32,128]{2,1,0:T(8,128)(2,1)S(1)}, bf16[16,32,128]{2,1,0:T(8,128)(2,1)S(1)}, bf16[16,5,64,128]{3,2,1,0:T(8,128)(2,1)}) custom-call(s32[2]{0:T(128)S(1)} %pad_add_fusion.place_ref, s32[8]{0:T(128)S(1)} %copy-done.3, bf16[16,144,128]{2,1,0:T(8,128)(2,1)S(1)} %copy-done, ...), custom_call_target="tpu_custom_call" | custom-call | tf_op jit(solution)/shard_map/pallas_call | solution.py:220
  66.7 0.7 copy-done.2
  67.3 19.1 %all-to-all-start.2 = ((bf16[16,5,64,128]{3,2,1,0:T(8,128)(2,1)}), bf16[16,5,64,128]{3,2,1,0:T(8,128)(2,1)S(1)}, u32[]{:S(2)}, u32[]{:S(2)}) async-start(bf16[16,5,64,128]{3,2,1,0:T(8,128)(2,1)} %get-tuple-element.16), calls=%async_computation.2 | async-start | bytes 2621440 | tf_op jit(solution)/shard_map/all_to_all | solution.py:255
  86.4 1.8 %collective-permute-start.3 = (bf16[16,32,128]{2,1,0:T(8,128)(2,1)S(1)}, bf16[16,32,128]{2,1,0:T(8,128)(2,1)S(1)}, u32[]{:S(2)}, u32[]{:S(2)}) collective-permute-start(bf16[16,32,128]{2,1,0:T(8,128)(2,1)S(1)} %get-tuple-element.13), channel_id=1, source_target_pairs={{0,1},{1,0},{2,3},{3,2},{4,5},{5,4},{6,7},{7,6},{8,9},{9,8},{10,11... | collective-permute-start | bytes 393224 | tf_op jit(solution)/shard_map/ppermute | solution.py:213
  88.2 0.0 collective-permute-start.4
  88.2 1.7 %collective-permute-start.5 = (bf16[16,32,128]{2,1,0:T(8,128)(2,1)S(1)}, bf16[16,32,128]{2,1,0:T(8,128)(2,1)S(1)}, u32[]{:S(2)}, u32[]{:S(2)}) collective-permute-start(bf16[16,32,128]{2,1,0:T(8,128)(2,1)S(1)} %get-tuple-element.15), channel_id=1, source_target_pairs={{0,3},{1,2},{2,1},{3,0},{4,7},{5,6},{6,5},{7,4},{8,11},{9,10},{10,... | collective-permute-start | bytes 393224 | tf_op jit(solution)/shard_map/ppermute | solution.py:213
  90.0 2.8 %collective-permute-done.3.dq1 = bf16[16,32,128]{2,1,0:T(8,128)(2,1)S(1)} collective-permute-done((bf16[16,32,128]{2,1,0:T(8,128)(2,1)S(1)}, bf16[16,32,128]{2,1,0:T(8,128)(2,1)S(1)}, u32[]{:S(2)}, u32[]{:S(2)}) %collective-permute-start.3) | collective-permute-done | bytes 131104 | tf_op jit(solution)/shard_map/ppermute | solution.py:213
  92.8 4.9 %collective-permute-done.4.dq2 = bf16[16,32,128]{2,1,0:T(8,128)(2,1)S(1)} collective-permute-done((bf16[16,32,128]{2,1,0:T(8,128)(2,1)S(1)}, bf16[16,32,128]{2,1,0:T(8,128)(2,1)S(1)}, u32[]{:S(2)}, u32[]{:S(2)}) %collective-permute-start.4) | collective-permute-done | bytes 131104 | tf_op jit(solution)/shard_map/ppermute | solution.py:213
  97.8 4.2 %collective-permute-done.5.dq3 = bf16[16,32,128]{2,1,0:T(8,128)(2,1)S(1)} collective-permute-done((bf16[16,32,128]{2,1,0:T(8,128)(2,1)S(1)}, bf16[16,32,128]{2,1,0:T(8,128)(2,1)S(1)}, u32[]{:S(2)}, u32[]{:S(2)}) %collective-permute-start.5) | collective-permute-done | bytes 131104 | tf_op jit(solution)/shard_map/ppermute | solution.py:213
  102.0 5.2 %all-to-all-done.2.dkv_ref = bf16[16,5,64,128]{3,2,1,0:T(8,128)(2,1)S(1)} async-done(((bf16[16,5,64,128]{3,2,1,0:T(8,128)(2,1)}), bf16[16,5,64,128]{3,2,1,0:T(8,128)(2,1)S(1)}, u32[]{:S(2)}, u32[]{:S(2)}) %all-to-all-start.2) | async-done | bytes 1310752 | tf_op jit(solution)/shard_map/all_to_all | solution.py:255
  107.2 0.0 copy-done.5
  107.2 0.0 copy-done.6
  107.2 0.0 copy-done.7
  107.2 1.1 copy-done.4
  108.3 2.5 %shard_map.97 = bf16[16,96,128]{2,1,0:T(8,128)(2,1)} custom-call(bf16[16,32,128]{2,1,0:T(8,128)(2,1)} %copy-done.2, bf16[16,32,128]{2,1,0:T(8,128)(2,1)} %copy-done.5, bf16[16,32,128]{2,1,0:T(8,128)(2,1)} %copy-done.6, bf16[16,32,128]{2,1,0:T(8,128)(2,1)} %copy-done.7, bf16[16,5,64,128]{3,2,1,0:T(8,128)(2,1)} %copy-done.4), custom_call_target="tpu_custom_call" | custom-call | tf_op jit(solution)/shard_map/pallas_call | solution.py:257
  110.8 19.8 %all_to_all.21.in_ref = bf16[16,96,128]{2,1,0:T(8,128)(2,1)} all-to-all(bf16[16,96,128]{2,1,0:T(8,128)(2,1)} %shard_map.97), channel_id=1, replica_groups=mesh['qrow'=16,'kcol_h'=4,'kcol_s'=4] {'kcol_h','kcol_s'}, dimensions={0} | all-to-all | bytes 786432 | tf_op jit(solution)/shard_map/all_to_all | solution.py:263
  130.6 1.8 %shard_map.98 = (bf16[128,512]{1,0:T(8,128)(2,1)}, bf16[128,512]{1,0:T(8,128)(2,1)}, bf16[128,512]{1,0:T(8,128)(2,1)}) custom-call(bf16[16,96,128]{2,1,0:T(8,128)(2,1)} %all_to_all.21.in_ref), custom_call_target="tpu_custom_call" | custom-call | tf_op jit(solution)/shard_map/pallas_call | solution.py:266
  (8 shorter events, 0.0 us)
Async XLA Ops:
  32.4 6.3 %copy-start.1 = (bf16[16,64,128]{2,1,0:T(8,128)(2,1)S(1)}, bf16[16,64,128]{2,1,0:T(8,128)(2,1)}, u32[]{:S(2)}) copy-start(bf16[16,64,128]{2,1,0:T(8,128)(2,1)} %get-tuple-element.10.qg0) | copy-start | bytes 786436
  32.4 29.1 %copy-start = (bf16[16,144,128]{2,1,0:T(8,128)(2,1)S(1)}, bf16[16,144,128]{2,1,0:T(8,128)(2,1)}, u32[]{:S(2)}) copy-start(bf16[16,144,128]{2,1,0:T(8,128)(2,1)} %all_to_all.20.in_ref) | copy-start | bytes 1769476
  32.4 29.1 %copy-start.3 = (s32[8]{0:T(128)S(1)}, s32[8]{0:T(128)}, u32[]{:S(2)}) copy-start(s32[8]{0:T(128)} %lengths_ref.1) | copy-start | bytes 100
  32.4 29.0 %all-to-all-start.1 = ((bf16[16,5,64,128]{3,2,1,0:T(8,128)(2,1)}), bf16[16,5,64,128]{3,2,1,0:T(8,128)(2,1)S(1)}, u32[]{:S(2)}, u32[]{:S(2)}) async-start(bf16[16,5,64,128]{3,2,1,0:T(8,128)(2,1)} %get-tuple-element.11), calls=%async_computation.1 | async-start | bytes 2621440 | tf_op jit(solution)/shard_map/all_to_all | solution.py:251
  38.7 12.6 %collective-permute-start.1 = (bf16[16,64,128]{2,1,0:T(8,128)(2,1)S(1)}, bf16[16,64,128]{2,1,0:T(8,128)(2,1)S(1)}, u32[]{:S(2)}, u32[]{:S(2)}) collective-permute-start(bf16[16,64,128]{2,1,0:T(8,128)(2,1)S(1)} %copy-done.1), channel_id=1, source_target_pairs={{0,2},{1,3},{2,0},{3,1},{4,6},{5,7},{6,4},{7,5},{8,10},{9,11},{10,... | collective-permute-start | bytes 786440 | tf_op jit(solution)/shard_map/ppermute | solution.py:213
  39.5 15.8 %collective-permute-start = (bf16[16,64,128]{2,1,0:T(8,128)(2,1)S(1)}, bf16[16,64,128]{2,1,0:T(8,128)(2,1)S(1)}, u32[]{:S(2)}, u32[]{:S(2)}) collective-permute-start(bf16[16,64,128]{2,1,0:T(8,128)(2,1)S(1)} %copy-done.1), channel_id=1, source_target_pairs={{0,1},{1,0},{2,3},{3,2},{4,5},{5,4},{6,7},{7,6},{8,9},{9,8},{10,11... | collective-permute-start | bytes 786440 | tf_op jit(solution)/shard_map/ppermute | solution.py:213
  51.3 10.2 %collective-permute-start.2 = (bf16[16,64,128]{2,1,0:T(8,128)(2,1)S(1)}, bf16[16,64,128]{2,1,0:T(8,128)(2,1)S(1)}, u32[]{:S(2)}, u32[]{:S(2)}) collective-permute-start(bf16[16,64,128]{2,1,0:T(8,128)(2,1)S(1)} %collective-permute-done.1.qg2), channel_id=1, source_target_pairs={{0,1},{1,0},{2,3},{3,2},{4,5},{5,4},{6,7},{7,6},{8,9},{9,8},{10,11... | collective-permute-start | bytes 786440 | tf_op jit(solution)/shard_map/ppermute | solution.py:213
  66.7 0.7 copy-start.2
  67.3 39.9 %all-to-all-start.2 = ((bf16[16,5,64,128]{3,2,1,0:T(8,128)(2,1)}), bf16[16,5,64,128]{3,2,1,0:T(8,128)(2,1)S(1)}, u32[]{:S(2)}, u32[]{:S(2)}) async-start(bf16[16,5,64,128]{3,2,1,0:T(8,128)(2,1)} %get-tuple-element.16), calls=%async_computation.2 | async-start | bytes 2621440 | tf_op jit(solution)/shard_map/all_to_all | solution.py:255
  86.4 6.4 %collective-permute-start.3 = (bf16[16,32,128]{2,1,0:T(8,128)(2,1)S(1)}, bf16[16,32,128]{2,1,0:T(8,128)(2,1)S(1)}, u32[]{:S(2)}, u32[]{:S(2)}) collective-permute-start(bf16[16,32,128]{2,1,0:T(8,128)(2,1)S(1)} %get-tuple-element.13), channel_id=1, source_target_pairs={{0,1},{1,0},{2,3},{3,2},{4,5},{5,4},{6,7},{7,6},{8,9},{9,8},{10,11... | collective-permute-start | bytes 393224 | tf_op jit(solution)/shard_map/ppermute | solution.py:213
  88.2 9.5 %collective-permute-start.4 = (bf16[16,32,128]{2,1,0:T(8,128)(2,1)S(1)}, bf16[16,32,128]{2,1,0:T(8,128)(2,1)S(1)}, u32[]{:S(2)}, u32[]{:S(2)}) collective-permute-start(bf16[16,32,128]{2,1,0:T(8,128)(2,1)S(1)} %get-tuple-element.14), channel_id=1, source_target_pairs={{0,2},{1,3},{2,0},{3,1},{4,6},{5,7},{6,4},{7,5},{8,10},{9,11},{10,... | collective-permute-start | bytes 393224 | tf_op jit(solution)/shard_map/ppermute | solution.py:213
  88.2 13.7 %collective-permute-start.5 = (bf16[16,32,128]{2,1,0:T(8,128)(2,1)S(1)}, bf16[16,32,128]{2,1,0:T(8,128)(2,1)S(1)}, u32[]{:S(2)}, u32[]{:S(2)}) collective-permute-start(bf16[16,32,128]{2,1,0:T(8,128)(2,1)S(1)} %get-tuple-element.15), channel_id=1, source_target_pairs={{0,3},{1,2},{2,1},{3,0},{4,7},{5,6},{6,5},{7,4},{8,11},{9,10},{10,... | collective-permute-start | bytes 393224 | tf_op jit(solution)/shard_map/ppermute | solution.py:213
  92.8 14.4 %copy-start.5 = (bf16[16,32,128]{2,1,0:T(8,128)(2,1)}, bf16[16,32,128]{2,1,0:T(8,128)(2,1)S(1)}, u32[]{:S(2)}) copy-start(bf16[16,32,128]{2,1,0:T(8,128)(2,1)S(1)} %collective-permute-done.3.dq1) | copy-start | bytes 393220
  97.7 9.5 %copy-start.6 = (bf16[16,32,128]{2,1,0:T(8,128)(2,1)}, bf16[16,32,128]{2,1,0:T(8,128)(2,1)S(1)}, u32[]{:S(2)}) copy-start(bf16[16,32,128]{2,1,0:T(8,128)(2,1)S(1)} %collective-permute-done.4.dq2) | copy-start | bytes 393220
  102.0 5.2 %copy-start.7 = (bf16[16,32,128]{2,1,0:T(8,128)(2,1)}, bf16[16,32,128]{2,1,0:T(8,128)(2,1)S(1)}, u32[]{:S(2)}) copy-start(bf16[16,32,128]{2,1,0:T(8,128)(2,1)S(1)} %collective-permute-done.5.dq3) | copy-start | bytes 393220
  107.2 1.1 copy-start.4

commit v3 on v2

--- a/solution.py
+++ b/solution.py
@@ -20,7 +20,7 @@
 QROWS = 1024
 SCALE = HEAD_DIM**-0.5
 LOG2E = math.log2(math.e)
-EXTRA = 16
+EXTRA = 8
 OFF_DO = STRIP
 OFF_K = 2 * STRIP
 OFF_V = 3 * STRIP
@@ -31,6 +31,7 @@
 F32 = jnp.float32
 BF16 = jnp.bfloat16
 VMEM = pl.BlockSpec(memory_space=pltpu.VMEM)
+SMALL = pltpu.CompilerParams(vmem_limit_bytes=8 * 1024 * 1024)
 SMEM = pl.BlockSpec(memory_space=pltpu.SMEM)
 
 
@@ -227,7 +228,7 @@
             pltpu.VMEM((tiles, KROWS, HEAD_DIM), F32),
             pltpu.VMEM((HEAD_DIM, QROWS), F32),
         ] + [pltpu.VMEM((ways, WAYS, STRIP, HEAD_DIM), BF16)] * 3,
-        compiler_params=pltpu.CompilerParams(vmem_limit_bytes=40 * 1024 * 1024),
+        compiler_params=pltpu.CompilerParams(vmem_limit_bytes=24 * 1024 * 1024),
     )(place, doc_lengths, mine, qg, *rest)
 
 
@@ -237,6 +238,7 @@
     place = jnp.stack([lax.axis_index("qrow"), lax.axis_index(STRIPS)]).astype(jnp.int32)
     packed = pl.pallas_call(
         pack_kernel,
+        compiler_params=pltpu.CompilerParams(vmem_limit_bytes=60 * 1024 * 1024),
         in_specs=[VMEM] * 6,
         out_specs=VMEM,
         out_shape=shape(ways, PACKED, HEAD_DIM),
@@ -244,6 +246,7 @@
     mine = lax.all_to_all(packed, KCOL, 0, 0)
     spread, qg = pl.pallas_call(
         spread_kernel,
+        compiler_params=SMALL,
         in_specs=[VMEM],
         out_specs=[VMEM] * 2,
         out_shape=[shape(blocks, REACH, 2 * STRIP, HEAD_DIM), shape(ways, 2 * STRIP, HEAD_DIM)],
@@ -256,6 +259,7 @@
     dq_parts = [dq_parts[0]] + [from_partner(dq_parts[s], s) for s in range(1, WAYS)]
     sums = pl.pallas_call(
         collect_kernel,
+        compiler_params=SMALL,
         in_specs=[VMEM] * 5,
         out_specs=VMEM,
         out_shape=shape(ways, 3 * STRIP, HEAD_DIM),
@@ -265,6 +269,7 @@
     return tuple(
         pl.pallas_call(
             unpack_kernel,
+            compiler_params=SMALL,
             in_specs=[VMEM],
             out_specs=[VMEM] * 3,
             out_shape=[shape(CHUNK, width)] * 3,

time: 130 us -> 120 us (0.923)
  Pallas kernels: 14.4 us -> 9.97 us
  starting transfers between devices: 35 us -> 32.7 us
  blocking collectives: 46.7 us -> 44.5 us
  local copies, waits for them, and re-layouts: 1.75 us -> 0.01 us
    pallas_call x4, Pallas kernels: 9.21 us -> 4.79 us  [the longest x1 2.51 us: per_device(): pl.pallas_call(pack_kernel, compiler_params=pltpu.CompilerParams(vmem_lim...]
    all_to_all x1, starting transfers between devices: 19.1 us -> 16.7 us  [per_device(): dkv = lax.all_to_all(dkv_part, 'qrow', 0, 0)]
    unnamed x16 -> x2, local copies, waits for them, and re-layouts: 1.75 us -> 0.01 us
    all_to_all x1, blocking collectives: 19.8 us -> 18.3 us  [per_device(): back = lax.all_to_all(sums, KCOL, 0, 0)]
where the time goes in v3:
time: 120 us; the launch traced here: 122 us
  blocking collectives  44.5 us (37%)
  waiting for transfers between devices  33.8 us (28%)
  starting transfers between devices  32.7 us (27%)
  Pallas kernels  9.97 us (8%)
    ppermute x6, waiting for transfers between devices, from_partner(): return lax.ppermute(x, STRIPS, [(d, d ^ s) for d in range(WAYS)])  28.6 us
    all_to_all x1, blocking collectives, per_device(): mine = lax.all_to_all(packed, KCOL, 0, 0)  26.2 us
    all_to_all x1, blocking collectives, per_device(): back = lax.all_to_all(sums, KCOL, 0, 0)  18.3 us
    all_to_all x1, starting transfers between devices, per_device(): dkv = lax.all_to_all(dkv_part, 'qrow', 0, 0)  16.7 us
    ppermute x6, starting transfers between devices, from_partner(): return lax.ppermute(x, STRIPS, [(d, d ^ s) for d in range(WAYS)])  9.78 us
    all_to_all x1, starting transfers between devices, per_device(): keys = lax.all_to_all(spread, 'qrow', 0, 0)  6.27 us
    all_to_all x1, waiting for transfers between devices, per_device(): dkv = lax.all_to_all(dkv_part, 'qrow', 0, 0)  5.23 us
    pallas_call x1, Pallas kernels, call_tiles(): pl.pallas_call(tiles_kernel, in_specs=[SMEM, SMEM] + [VMEM] * 6, out_spec...  5.18 us
  transfers between devices with their start and end apart: 8, of which 6 were waited for; matrix products, arithmetic and copies ran while one was open for 0% of the time, Pallas kernels for 0%

profile of v3, /device:TPU:40, one launch (start us, length us, event | category | flops | bytes accessed | tf_op | source)
XLA Modules:
  0.0 121.7 jit_solution(9871819256717346093)
XLA Ops:
  0.6 2.5 %shard_map.94 = bf16[16,136,128]{2,1,0:T(8,128)(2,1)} custom-call(bf16[128,512]{1,0:T(8,128)(2,1)} %q_ref.1, bf16[128,512]{1,0:T(8,128)(2,1)} %k_ref.1, bf16[128,512]{1,0:T(8,128)(2,1)} %v_ref.1, bf16[128,512]{1,0:T(8,128)(2,1)} %o_ref.1, bf16[128,512]{1,0:T(8,128)(2,1)} %g_ref.1, f32[4,128]{1,0:T(4,128)} %bitcast.3), custom_call_target="tpu_custom_call" | custom-call | tf_op jit(solution)/shard_map/pallas_call | solution.py:239
  3.1 26.2 %all_to_all.20.in_ref = bf16[16,136,128]{2,1,0:T(8,128)(2,1)S(1)} all-to-all(bf16[16,136,128]{2,1,0:T(8,128)(2,1)} %shard_map.94), channel_id=1, replica_groups=mesh['qrow'=16,'kcol_h'=4,'kcol_s'=4] {'kcol_h','kcol_s'}, dimensions={0} | all-to-all | bytes 1114112 | tf_op jit(solution)/shard_map/all_to_all | solution.py:246
  29.3 1.3 %shard_map.95 = (bf16[16,5,64,128]{3,2,1,0:T(8,128)(2,1)}, bf16[16,64,128]{2,1,0:T(8,128)(2,1)S(1)}) custom-call(bf16[16,136,128]{2,1,0:T(8,128)(2,1)S(1)} %all_to_all.20.in_ref), custom_call_target="tpu_custom_call" | custom-call | tf_op jit(solution)/shard_map/pallas_call | solution.py:247
  30.6 0.0 copy-start
  30.6 6.3 %all-to-all-start.1 = ((bf16[16,5,64,128]{3,2,1,0:T(8,128)(2,1)}), bf16[16,5,64,128]{3,2,1,0:T(8,128)(2,1)S(1)}, u32[]{:S(2)}, u32[]{:S(2)}) async-start(bf16[16,5,64,128]{3,2,1,0:T(8,128)(2,1)} %get-tuple-element.11), calls=%async_computation.1 | async-start | bytes 2621440 | tf_op jit(solution)/shard_map/all_to_all | solution.py:254
  36.9 0.7 collective-permute-start.1
  37.6 1.4 %collective-permute-start = (bf16[16,64,128]{2,1,0:T(8,128)(2,1)S(1)}, bf16[16,64,128]{2,1,0:T(8,128)(2,1)S(1)}, u32[]{:S(2)}, u32[]{:S(2)}) collective-permute-start(bf16[16,64,128]{2,1,0:T(8,128)(2,1)S(1)} %get-tuple-element.10.qg0), channel_id=1, source_target_pairs={{0,1},{1,0},{2,3},{3,2},{4,5},{5,4},{6,7},{7,6},{8,9},{9,8},{10,11... | collective-permute-start | bytes 786440 | tf_op jit(solution)/shard_map/ppermute | solution.py:214
  39.0 10.3 %collective-permute-done.1.qg2 = bf16[16,64,128]{2,1,0:T(8,128)(2,1)S(1)} collective-permute-done((bf16[16,64,128]{2,1,0:T(8,128)(2,1)S(1)}, bf16[16,64,128]{2,1,0:T(8,128)(2,1)S(1)}, u32[]{:S(2)}, u32[]{:S(2)}) %collective-permute-start.1) | collective-permute-done | bytes 262176 | tf_op jit(solution)/shard_map/ppermute | solution.py:214
  49.3 4.1 %collective-permute-start.2 = (bf16[16,64,128]{2,1,0:T(8,128)(2,1)S(1)}, bf16[16,64,128]{2,1,0:T(8,128)(2,1)S(1)}, u32[]{:S(2)}, u32[]{:S(2)}) collective-permute-start(bf16[16,64,128]{2,1,0:T(8,128)(2,1)S(1)} %collective-permute-done.1.qg2), channel_id=1, source_target_pairs={{0,1},{1,0},{2,3},{3,2},{4,5},{5,4},{6,7},{7,6},{8,9},{9,8},{10,11... | collective-permute-start | bytes 786440 | tf_op jit(solution)/shard_map/ppermute | solution.py:214
  53.3 0.1 pad_add_fusion.place_ref
  53.4 0.0 collective-permute-done.qg1
  53.4 6.3 %collective-permute-done.2.qg3 = bf16[16,64,128]{2,1,0:T(8,128)(2,1)S(1)} collective-permute-done((bf16[16,64,128]{2,1,0:T(8,128)(2,1)S(1)}, bf16[16,64,128]{2,1,0:T(8,128)(2,1)S(1)}, u32[]{:S(2)}, u32[]{:S(2)}) %collective-permute-start.2) | collective-permute-done | bytes 262176 | tf_op jit(solution)/shard_map/ppermute | solution.py:214
  59.7 0.0 all-to-all-done.1.kv_ref
  59.7 0.0 copy-done
  59.7 5.2 %shard_map.96 = (bf16[16,32,128]{2,1,0:T(8,128)(2,1)S(1)}, bf16[16,32,128]{2,1,0:T(8,128)(2,1)S(1)}, bf16[16,32,128]{2,1,0:T(8,128)(2,1)S(1)}, bf16[16,32,128]{2,1,0:T(8,128)(2,1)S(1)}, bf16[16,5,64,128]{3,2,1,0:T(8,128)(2,1)}) custom-call(s32[2]{0:T(128)S(1)} %pad_add_fusion.place_ref, s32[8]{0:T(128)S(1)} %copy-done, ...), custom_call_target="tpu_custom_call" | custom-call | tf_op jit(solution)/shard_map/pallas_call | solution.py:221
  64.9 16.7 %all-to-all-start.2 = ((bf16[16,5,64,128]{3,2,1,0:T(8,128)(2,1)}), bf16[16,5,64,128]{3,2,1,0:T(8,128)(2,1)S(1)}, u32[]{:S(2)}, u32[]{:S(2)}) async-start(bf16[16,5,64,128]{3,2,1,0:T(8,128)(2,1)} %get-tuple-element.16), calls=%async_computation.2 | async-start | bytes 2621440 | tf_op jit(solution)/shard_map/all_to_all | solution.py:258
  81.6 1.8 %collective-permute-start.3 = (bf16[16,32,128]{2,1,0:T(8,128)(2,1)S(1)}, bf16[16,32,128]{2,1,0:T(8,128)(2,1)S(1)}, u32[]{:S(2)}, u32[]{:S(2)}) collective-permute-start(bf16[16,32,128]{2,1,0:T(8,128)(2,1)S(1)} %get-tuple-element.13), channel_id=1, source_target_pairs={{0,1},{1,0},{2,3},{3,2},{4,5},{5,4},{6,7},{7,6},{8,9},{9,8},{10,11... | collective-permute-start | bytes 393224 | tf_op jit(solution)/shard_map/ppermute | solution.py:214
  83.4 0.0 collective-permute-start.4
  83.4 1.7 %collective-permute-start.5 = (bf16[16,32,128]{2,1,0:T(8,128)(2,1)S(1)}, bf16[16,32,128]{2,1,0:T(8,128)(2,1)S(1)}, u32[]{:S(2)}, u32[]{:S(2)}) collective-permute-start(bf16[16,32,128]{2,1,0:T(8,128)(2,1)S(1)} %get-tuple-element.15), channel_id=1, source_target_pairs={{0,3},{1,2},{2,1},{3,0},{4,7},{5,6},{6,5},{7,4},{8,11},{9,10},{10,... | collective-permute-start | bytes 393224 | tf_op jit(solution)/shard_map/ppermute | solution.py:214
  85.2 2.8 %collective-permute-done.3.dq1 = bf16[16,32,128]{2,1,0:T(8,128)(2,1)S(1)} collective-permute-done((bf16[16,32,128]{2,1,0:T(8,128)(2,1)S(1)}, bf16[16,32,128]{2,1,0:T(8,128)(2,1)S(1)}, u32[]{:S(2)}, u32[]{:S(2)}) %collective-permute-start.3) | collective-permute-done | bytes 131104 | tf_op jit(solution)/shard_map/ppermute | solution.py:214
  88.0 4.9 %collective-permute-done.4.dq2 = bf16[16,32,128]{2,1,0:T(8,128)(2,1)S(1)} collective-permute-done((bf16[16,32,128]{2,1,0:T(8,128)(2,1)S(1)}, bf16[16,32,128]{2,1,0:T(8,128)(2,1)S(1)}, u32[]{:S(2)}, u32[]{:S(2)}) %collective-permute-start.4) | collective-permute-done | bytes 131104 | tf_op jit(solution)/shard_map/ppermute | solution.py:214
  92.9 4.2 %collective-permute-done.5.dq3 = bf16[16,32,128]{2,1,0:T(8,128)(2,1)S(1)} collective-permute-done((bf16[16,32,128]{2,1,0:T(8,128)(2,1)S(1)}, bf16[16,32,128]{2,1,0:T(8,128)(2,1)S(1)}, u32[]{:S(2)}, u32[]{:S(2)}) %collective-permute-start.5) | collective-permute-done | bytes 131104 | tf_op jit(solution)/shard_map/ppermute | solution.py:214
  97.2 5.2 %all-to-all-done.2.dkv_ref = bf16[16,5,64,128]{3,2,1,0:T(8,128)(2,1)S(1)} async-done(((bf16[16,5,64,128]{3,2,1,0:T(8,128)(2,1)}), bf16[16,5,64,128]{3,2,1,0:T(8,128)(2,1)S(1)}, u32[]{:S(2)}, u32[]{:S(2)}) %all-to-all-start.2) | async-done | bytes 1310752 | tf_op jit(solution)/shard_map/all_to_all | solution.py:258
  102.4 0.2 shard_map.97
  102.6 18.3 %all_to_all.21.in_ref = bf16[16,96,128]{2,1,0:T(8,128)(2,1)S(1)} all-to-all(bf16[16,96,128]{2,1,0:T(8,128)(2,1)S(1)} %shard_map.97), channel_id=1, replica_groups=mesh['qrow'=16,'kcol_h'=4,'kcol_s'=4] {'kcol_h','kcol_s'}, dimensions={0} | all-to-all | bytes 786432 | tf_op jit(solution)/shard_map/all_to_all | solution.py:267
  120.9 0.8 shard_map.98
Async XLA Ops:
  30.6 29.1 %copy-start = (s32[8]{0:T(128)S(1)}, s32[8]{0:T(128)}, u32[]{:S(2)}) copy-start(s32[8]{0:T(128)} %lengths_ref.1) | copy-start | bytes 100
  30.6 29.1 %all-to-all-start.1 = ((bf16[16,5,64,128]{3,2,1,0:T(8,128)(2,1)}), bf16[16,5,64,128]{3,2,1,0:T(8,128)(2,1)S(1)}, u32[]{:S(2)}, u32[]{:S(2)}) async-start(bf16[16,5,64,128]{3,2,1,0:T(8,128)(2,1)} %get-tuple-element.11), calls=%async_computation.1 | async-start | bytes 2621440 | tf_op jit(solution)/shard_map/all_to_all | solution.py:254
  36.9 12.4 %collective-permute-start.1 = (bf16[16,64,128]{2,1,0:T(8,128)(2,1)S(1)}, bf16[16,64,128]{2,1,0:T(8,128)(2,1)S(1)}, u32[]{:S(2)}, u32[]{:S(2)}) collective-permute-start(bf16[16,64,128]{2,1,0:T(8,128)(2,1)S(1)} %get-tuple-element.10.qg0), channel_id=1, source_target_pairs={{0,2},{1,3},{2,0},{3,1},{4,6},{5,7},{6,4},{7,5},{8,10},{9,11},{10,... | collective-permute-start | bytes 786440 | tf_op jit(solution)/shard_map/ppermute | solution.py:214
  37.6 15.9 %collective-permute-start = (bf16[16,64,128]{2,1,0:T(8,128)(2,1)S(1)}, bf16[16,64,128]{2,1,0:T(8,128)(2,1)S(1)}, u32[]{:S(2)}, u32[]{:S(2)}) collective-permute-start(bf16[16,64,128]{2,1,0:T(8,128)(2,1)S(1)} %get-tuple-element.10.qg0), channel_id=1, source_target_pairs={{0,1},{1,0},{2,3},{3,2},{4,5},{5,4},{6,7},{7,6},{8,9},{9,8},{10,11... | collective-permute-start | bytes 786440 | tf_op jit(solution)/shard_map/ppermute | solution.py:214
  49.3 10.4 %collective-permute-start.2 = (bf16[16,64,128]{2,1,0:T(8,128)(2,1)S(1)}, bf16[16,64,128]{2,1,0:T(8,128)(2,1)S(1)}, u32[]{:S(2)}, u32[]{:S(2)}) collective-permute-start(bf16[16,64,128]{2,1,0:T(8,128)(2,1)S(1)} %collective-permute-done.1.qg2), channel_id=1, source_target_pairs={{0,1},{1,0},{2,3},{3,2},{4,5},{5,4},{6,7},{7,6},{8,9},{9,8},{10,11... | collective-permute-start | bytes 786440 | tf_op jit(solution)/shard_map/ppermute | solution.py:214
  64.9 37.5 %all-to-all-start.2 = ((bf16[16,5,64,128]{3,2,1,0:T(8,128)(2,1)}), bf16[16,5,64,128]{3,2,1,0:T(8,128)(2,1)S(1)}, u32[]{:S(2)}, u32[]{:S(2)}) async-start(bf16[16,5,64,128]{3,2,1,0:T(8,128)(2,1)} %get-tuple-element.16), calls=%async_computation.2 | async-start | bytes 2621440 | tf_op jit(solution)/shard_map/all_to_all | solution.py:258
  81.6 6.4 %collective-permute-start.3 = (bf16[16,32,128]{2,1,0:T(8,128)(2,1)S(1)}, bf16[16,32,128]{2,1,0:T(8,128)(2,1)S(1)}, u32[]{:S(2)}, u32[]{:S(2)}) collective-permute-start(bf16[16,32,128]{2,1,0:T(8,128)(2,1)S(1)} %get-tuple-element.13), channel_id=1, source_target_pairs={{0,1},{1,0},{2,3},{3,2},{4,5},{5,4},{6,7},{7,6},{8,9},{9,8},{10,11... | collective-permute-start | bytes 393224 | tf_op jit(solution)/shard_map/ppermute | solution.py:214
  83.4 9.5 %collective-permute-start.4 = (bf16[16,32,128]{2,1,0:T(8,128)(2,1)S(1)}, bf16[16,32,128]{2,1,0:T(8,128)(2,1)S(1)}, u32[]{:S(2)}, u32[]{:S(2)}) collective-permute-start(bf16[16,32,128]{2,1,0:T(8,128)(2,1)S(1)} %get-tuple-element.14), channel_id=1, source_target_pairs={{0,2},{1,3},{2,0},{3,1},{4,6},{5,7},{6,4},{7,5},{8,10},{9,11},{10,... | collective-permute-start | bytes 393224 | tf_op jit(solution)/shard_map/ppermute | solution.py:214
  83.4 13.7 %collective-permute-start.5 = (bf16[16,32,128]{2,1,0:T(8,128)(2,1)S(1)}, bf16[16,32,128]{2,1,0:T(8,128)(2,1)S(1)}, u32[]{:S(2)}, u32[]{:S(2)}) collective-permute-start(bf16[16,32,128]{2,1,0:T(8,128)(2,1)S(1)} %get-tuple-element.15), channel_id=1, source_target_pairs={{0,3},{1,2},{2,1},{3,0},{4,7},{5,6},{6,5},{7,4},{8,11},{9,10},{10,... | collective-permute-start | bytes 393224 | tf_op jit(solution)/shard_map/ppermute | solution.py:214

commit v4 on v3

--- a/solution.py
+++ b/solution.py
@@ -15,9 +15,9 @@
 WAYS = 4
 STRIP = CHUNK // WAYS
 REACH = 5
-KSPAN = 1024
+KSPAN = 2048
 KROWS = KSPAN // WAYS
-QROWS = 1024
+QROWS = 512
 SCALE = HEAD_DIM**-0.5
 LOG2E = math.log2(math.e)
 EXTRA = 8
@@ -61,7 +61,7 @@
             jnp.concatenate(
                 [p.astype(F32) for p in pieces(norms[h : h + 1]) + pieces(delta)]
                 + [jnp.zeros((EXTRA - 6, CHUNK), F32)], axis=0
-            ).astype(BF16)
+            )
         )
     for t in range(out_ref.shape[0]):
         h, d = head_and_strip(t)
@@ -71,7 +71,8 @@
         out_ref[t, OFF_DO : OFF_DO + STRIP] = g_ref[rows, at]
         out_ref[t, OFF_K : OFF_K + STRIP] = k_ref[rows, at]
         out_ref[t, OFF_V : OFF_V + STRIP] = v_ref[rows, at]
-        out_ref[t, OFF_EXTRA:PACKED] = extras[h]
+        order = [extras[h][:, (d ^ s) * STRIP : (d ^ s) * STRIP + STRIP] for s in range(WAYS)]
+        out_ref[t, OFF_EXTRA:PACKED] = jnp.concatenate(order, axis=1).astype(BF16)
 
 
 def spread_kernel(in_ref, out_ref, qg_ref):
@@ -82,10 +83,7 @@
             out_ref[b, back] = in_ref[max(b - back, 0), OFF_K : OFF_K + 2 * STRIP]
 
 
-def tiles_kernel(
-    place_ref, lengths_ref, in_ref, qg0, qg1, qg2, qg3, kv_ref,
-    dq0, dq1, dq2, dq3, dkv_ref, dk_acc, dv_acc, dq_acc, q_all, g_all, dq_all,
-):
+def tiles(half, place_ref, lengths_ref, in_ref, qg_refs, kv_ref, dq_refs, dk_acc, dv_acc, dq_acc, q_all, g_all):
     block = place_ref[0]
     strip = place_ref[1]
     ends = []
@@ -94,92 +92,117 @@
         total = total + lengths_ref[e]
         ends.append(total)
     base = (block - (REACH - 1)) * BLOCK
-    for s, ref in enumerate((qg0, qg1, qg2, qg3)):
-        q_all[:, strip ^ s] = ref[:, 0:STRIP]
-        g_all[:, strip ^ s] = ref[:, STRIP : 2 * STRIP]
+    for i, ref in enumerate(qg_refs):
+        q_all[:, i] = ref[:, 0:STRIP]
+        g_all[:, i] = ref[:, STRIP : 2 * STRIP]
     dk_acc[...] = jnp.zeros_like(dk_acc)
     dv_acc[...] = jnp.zeros_like(dv_acc)
-    m_tile = QROWS // CHUNK
     j_tile = KROWS // STRIP
     per_block = BLOCK // KSPAN
     k_iota = lax.broadcasted_iota(jnp.int32, (KROWS, 1), 0)
     k_iota = (k_iota // STRIP) * CHUNK + k_iota % STRIP + strip * STRIP
-
-    def query_tile(t, carry):
-        first = block * BLOCK + t * QROWS
-        last = first + QROWS - 1
-        doc_first = jnp.int32(0)
-        doc_last = jnp.int32(0)
-        q_pos = first + lax.broadcasted_iota(jnp.int32, (1, QROWS), 1)
-        q_doc = jnp.zeros((1, QROWS), jnp.int32)
-        for end in ends:
-            doc_first = jnp.where(end <= first, end, doc_first)
-            doc_last = jnp.where(end <= last, end, doc_last)
-            q_doc = jnp.where(end <= q_pos, end, q_doc)
-        low = (doc_first - base) // KSPAN
-        high = (last - base) // KSPAN
-        q = q_all[pl.ds(t * m_tile, m_tile)].reshape(QROWS, HEAD_DIM)
-        g = g_all[pl.ds(t * m_tile, m_tile)].reshape(QROWS, HEAD_DIM)
-        extra = in_ref[pl.ds(t * m_tile, m_tile), OFF_EXTRA:PACKED].astype(F32)
-
-        def row(at):
-            parts = [
-                extra[m, at : at + 1] + extra[m, at + 1 : at + 2] + extra[m, at + 2 : at + 3]
-                for m in range(m_tile)
-            ]
-            return jnp.concatenate(parts, axis=1)
-
-        norm, delta = row(0), row(3)
-        dq_acc[...] = jnp.zeros_like(dq_acc)
-
-        def one_tile(kt, masked):
-            js = pl.ds((kt % per_block) * j_tile, j_tile)
-            back = REACH - 1 - kt // per_block
-            k = kv_ref[js, back, 0:STRIP].reshape(KROWS, HEAD_DIM)
-            v = kv_ref[js, back, STRIP : 2 * STRIP].reshape(KROWS, HEAD_DIM)
-            across = (((1,), (1,)), ((), ()))
-            s = lax.dot_general(k, q, across, preferred_element_type=F32)
-            p = jnp.exp2(s * (SCALE * LOG2E) - norm)
-            if masked:
-                k_pos = k_iota + (base + kt * KSPAN)
-                p = jnp.where((k_pos <= q_pos) & (k_pos >= q_doc), p, 0.0)
-            dp = lax.dot_general(v, g, across, preferred_element_type=F32)
-            ds = (p * (dp - delta)).astype(BF16)
-            p = p.astype(BF16)
-            dv_acc[kt] += jnp.dot(p, g, preferred_element_type=F32)
-            dk_acc[kt] += jnp.dot(ds, q, preferred_element_type=F32)
-            dq_acc[...] += lax.dot_general(
-                k, ds, (((0,), (0,)), ((), ())), preferred_element_type=F32
-            )
-
-        def key_tile(kt, carry):
-            start = base + kt * KSPAN
-            whole = (start + KSPAN - 1 <= first) & (start >= doc_last)
-
-            @pl.when(whole)
-            def _():
-                one_tile(kt, False)
-
-            @pl.when(jnp.logical_not(whole))
-            def _():
-                one_tile(kt, True)
-
-            return carry
-
-        lax.fori_loop(low, high + 1, key_tile, 0)
-        dq_all[pl.ds(t * m_tile, m_tile)] = (
-            (dq_acc[...].T * SCALE).astype(BF16).reshape(m_tile, WAYS, STRIP, HEAD_DIM)
+    for t in range(2 * STRIP * in_ref.shape[0] // QROWS):
+        query_tile(half, t, block, strip, ends, base, k_iota, in_ref, kv_ref, dq_refs, dk_acc, dv_acc, dq_acc, q_all, g_all)
+
+
+def query_tile(
+    half, t, block, strip, ends, base, k_iota, in_ref, kv_ref, dq_refs, dk_acc, dv_acc, dq_acc, q_all, g_all
+):
+    width = 2 * STRIP
+    sources = QROWS // width
+    ms = slice(t * sources, (t + 1) * sources)
+    span = sources * CHUNK
+    j_tile = KROWS // STRIP
+    per_block = BLOCK // KSPAN
+    dq_acc[...] = jnp.zeros_like(dq_acc)
+    first = block * BLOCK + t * span
+    last = first + span - 1
+    lane = lax.broadcasted_iota(jnp.int32, (1, QROWS), 1)
+    strips = [strip ^ (2 * half), strip ^ (2 * half + 1)]
+    q_pos = first + lane // width * CHUNK + lane % STRIP
+    q_pos = q_pos + jnp.where(lane // STRIP % 2 == 0, strips[0], strips[1]) * STRIP
+    q_doc = jnp.zeros((1, QROWS), jnp.int32)
+    doc_first = jnp.int32(0)
+    doc_last = jnp.int32(0)
+    for end in ends:
+        doc_first = jnp.where(end <= first, end, doc_first)
+        doc_last = jnp.where(end <= last, end, doc_last)
+        q_doc = jnp.where(end <= q_pos, end, q_doc)
+    low = (doc_first - base) // KSPAN
+    high = (last - base) // KSPAN
+    q = q_all[ms].reshape(QROWS, HEAD_DIM)
+    g = g_all[ms].reshape(QROWS, HEAD_DIM)
+
+    def row(at):
+        values = []
+        for m in range(t * sources, (t + 1) * sources):
+            e = in_ref[m, OFF_EXTRA:PACKED, half * width : (half + 1) * width].astype(F32)
+            values.append(e[at : at + 1] + e[at + 1 : at + 2] + e[at + 2 : at + 3])
+        return jnp.concatenate(values, axis=1)
+
+    norm, delta = row(0), row(3)
+
+    def one_tile(kt, masked):
+        js = pl.ds((kt % per_block) * j_tile, j_tile)
+        back = REACH - 1 - kt // per_block
+        k = kv_ref[js, back, 0:STRIP].reshape(KROWS, HEAD_DIM)
+        v = kv_ref[js, back, STRIP : 2 * STRIP].reshape(KROWS, HEAD_DIM)
+        across = (((1,), (1,)), ((), ()))
+        s = lax.dot_general(k, q, across, preferred_element_type=F32)
+        p = jnp.exp2(s * (SCALE * LOG2E) - norm)
+        if masked:
+            k_pos = k_iota + (base + kt * KSPAN)
+            p = jnp.where((k_pos <= q_pos) & (k_pos >= q_doc), p, 0.0)
+        dp = lax.dot_general(v, g, across, preferred_element_type=F32)
+        ds = (p * (dp - delta)).astype(BF16)
+        p = p.astype(BF16)
+        dv_acc[kt] += jnp.dot(p, g, preferred_element_type=F32)
+        dk_acc[kt] += jnp.dot(ds, q, preferred_element_type=F32)
+        dq_acc[...] += lax.dot_general(
+            k, ds, (((0,), (0,)), ((), ())), preferred_element_type=F32
         )
+
+    def key_tile(kt, carry):
+        start = base + kt * KSPAN
+        whole = (start + KSPAN - 1 <= first) & (start >= doc_last)
+
+        @pl.when(whole)
+        def _():
+            one_tile(kt, False)
+
+        @pl.when(jnp.logical_not(whole))
+        def _():
+            one_tile(kt, True)
+
         return carry
 
-    lax.fori_loop(0, BLOCK // QROWS, query_tile, 0)
-    for s, ref in enumerate((dq0, dq1, dq2, dq3)):
-        ref[...] = dq_all[:, strip ^ s]
+    lax.fori_loop(low, high + 1, key_tile, 0)
+    dq = (dq_acc[...].T * SCALE).astype(BF16).reshape(sources, 2, STRIP, HEAD_DIM)
+    for i, ref in enumerate(dq_refs):
+        ref[ms] = dq[:, i]
+
+
+def first_kernel(
+    place_ref, lengths_ref, in_ref, qg0, qg1, kv_ref,
+    dq0, dq1, dk_acc, dv_acc, dq_acc, q_all, g_all,
+):
+    tiles(0, place_ref, lengths_ref, in_ref, (qg0, qg1), kv_ref, (dq0, dq1), dk_acc, dv_acc, dq_acc, q_all, g_all)
+
+
+def second_kernel(
+    place_ref, lengths_ref, in_ref, qg2, qg3, kv_ref, dk_in, dv_in,
+    dq2, dq3, dkv_ref, dk_acc, dv_acc, dq_acc, q_all, g_all,
+):
+    tiles(1, place_ref, lengths_ref, in_ref, (qg2, qg3), kv_ref, (dq2, dq3), dk_acc, dv_acc, dq_acc, q_all, g_all)
+    j_tile = KROWS // STRIP
+    per_block = BLOCK // KSPAN
     for kt in range(REACH * per_block):
         js = slice((kt % per_block) * j_tile, (kt % per_block + 1) * j_tile)
         back = REACH - 1 - kt // per_block
-        dkv_ref[js, back, 0:STRIP] = (dk_acc[kt] * SCALE).astype(BF16).reshape(j_tile, STRIP, HEAD_DIM)
-        dkv_ref[js, back, STRIP : 2 * STRIP] = dv_acc[kt].astype(BF16).reshape(j_tile, STRIP, HEAD_DIM)
+        dk = (dk_acc[kt] + dk_in[kt]) * SCALE
+        dv = dv_acc[kt] + dv_in[kt]
+        dkv_ref[js, back, 0:STRIP] = dk.astype(BF16).reshape(j_tile, STRIP, HEAD_DIM)
+        dkv_ref[js, back, STRIP : 2 * STRIP] = dv.astype(BF16).reshape(j_tile, STRIP, HEAD_DIM)
 
 
 def collect_kernel(dq0, dq1, dq2, dq3, dkv_ref, out_ref):
@@ -214,22 +237,28 @@
     return lax.ppermute(x, STRIPS, [(d, d ^ s) for d in range(WAYS)])
 
 
-def call_tiles(place, doc_lengths, mine, qg, *rest):
-    keys = rest[-1]
+def call_tiles(place, doc_lengths, mine, own, near, far, diagonal, keys):
     ways, blocks = mine.shape[0], keys.shape[0]
-    tiles = REACH * BLOCK // KSPAN
-    return pl.pallas_call(
-        tiles_kernel,
+    sums = (REACH * BLOCK // KSPAN, KROWS, HEAD_DIM)
+    scratch = [pltpu.VMEM((HEAD_DIM, QROWS), F32)] + [pltpu.VMEM((ways, 2, STRIP, HEAD_DIM), BF16)] * 2
+    params = pltpu.CompilerParams(vmem_limit_bytes=24 * 1024 * 1024)
+    dq0, dq1, dk, dv = pl.pallas_call(
+        first_kernel,
+        in_specs=[SMEM, SMEM] + [VMEM] * 4,
+        out_specs=[VMEM] * 4,
+        out_shape=[shape(ways, STRIP, HEAD_DIM)] * 2 + [shape(*sums, dtype=F32)] * 2,
+        scratch_shapes=scratch,
+        compiler_params=params,
+    )(place, doc_lengths, mine, own, near, keys)
+    dq2, dq3, dkv = pl.pallas_call(
+        second_kernel,
         in_specs=[SMEM, SMEM] + [VMEM] * 6,
-        out_specs=[VMEM] * 5,
-        out_shape=[shape(ways, STRIP, HEAD_DIM)] * 4 + [shape(blocks, REACH, 2 * STRIP, HEAD_DIM)],
-        scratch_shapes=[
-            pltpu.VMEM((tiles, KROWS, HEAD_DIM), F32),
-            pltpu.VMEM((tiles, KROWS, HEAD_DIM), F32),
-            pltpu.VMEM((HEAD_DIM, QROWS), F32),
-        ] + [pltpu.VMEM((ways, WAYS, STRIP, HEAD_DIM), BF16)] * 3,
-        compiler_params=pltpu.CompilerParams(vmem_limit_bytes=24 * 1024 * 1024),
-    )(place, doc_lengths, mine, qg, *rest)
+        out_specs=[VMEM] * 3,
+        out_shape=[shape(ways, STRIP, HEAD_DIM)] * 2 + [shape(blocks, REACH, 2 * STRIP, HEAD_DIM)],
+        scratch_shapes=[pltpu.VMEM(sums, F32)] * 2 + scratch,
+        compiler_params=params,
+    )(place, doc_lengths, mine, far, diagonal, keys, dk, dv)
+    return dq0, dq1, dq2, dq3, dkv
 
 
 def per_device(query_states, key_states, value_states, saved_output, output_grad, normalizer, doc_lengths):

time: 120 us -> 117 us (0.975); the launches traced: 122 us -> 116 us
  starting transfers between devices: 32.7 us -> 27.8 us
  waiting for transfers between devices: 33.8 us -> 31.7 us
  Pallas kernels: 9.97 us -> 12 us
    ppermute x6, waiting for transfers between devices: 28.6 us -> 22.2 us  [from_partner(): return lax.ppermute(x, STRIPS, [(d, d ^ s) for d in range(WAYS)])]
    all_to_all x1, starting transfers between devices: 16.7 us -> 11.8 us  [per_device(): dkv = lax.all_to_all(dkv_part, 'qrow', 0, 0)]
    all_to_all x1, waiting for transfers between devices: 0.01 us -> 4.23 us  [per_device(): keys = lax.all_to_all(spread, 'qrow', 0, 0)]
    pallas_call x1 -> x2, Pallas kernels: 5.18 us -> 7.12 us  [the longest x1 4.22 us: call_tiles(): pl.pallas_call(second_kernel, in_specs=[SMEM, SMEM] + [VMEM] * 6, out_spe...]
  transfers between devices with their start and end apart: 8 -> 8, of which waited for: 6 -> 6; matrix products, arithmetic and copies ran while one was open for 0% -> 0% of each run, Pallas kernels for 0% -> 2%
where the time goes in v4:
time: 117 us; the launch traced here: 116 us
  blocking collectives  44.1 us (38%)
  waiting for transfers between devices  31.7 us (27%)
  starting transfers between devices  27.8 us (24%)
  Pallas kernels  12 us (10%)
    all_to_all x1, blocking collectives, per_device(): mine = lax.all_to_all(packed, KCOL, 0, 0)  26.2 us
    ppermute x6, waiting for transfers between devices, from_partner(): return lax.ppermute(x, STRIPS, [(d, d ^ s) for d in range(WAYS)])  22.2 us
    all_to_all x1, blocking collectives, per_device(): back = lax.all_to_all(sums, KCOL, 0, 0)  17.9 us
    all_to_all x1, starting transfers between devices, per_device(): dkv = lax.all_to_all(dkv_part, 'qrow', 0, 0)  11.8 us
    ppermute x6, starting transfers between devices, from_partner(): return lax.ppermute(x, STRIPS, [(d, d ^ s) for d in range(WAYS)])  9.78 us
    all_to_all x1, starting transfers between devices, per_device(): keys = lax.all_to_all(spread, 'qrow', 0, 0)  6.27 us
    all_to_all x1, waiting for transfers between devices, per_device(): dkv = lax.all_to_all(dkv_part, 'qrow', 0, 0)  5.32 us
    all_to_all x1, waiting for transfers between devices, per_device(): keys = lax.all_to_all(spread, 'qrow', 0, 0)  4.23 us
  transfers between devices with their start and end apart: 8, of which 6 were waited for; matrix products, arithmetic and copies ran while one was open for 0% of the time, Pallas kernels for 2%

profile of v4, /device:TPU:40, one launch (start us, length us, event | category | flops | bytes accessed | tf_op | source)
XLA Modules:
  0.0 116.4 jit_solution(336831220343116668)
XLA Ops:
  0.6 2.6 %shard_map.94 = bf16[16,136,128]{2,1,0:T(8,128)(2,1)} custom-call(bf16[128,512]{1,0:T(8,128)(2,1)} %q_ref.1, bf16[128,512]{1,0:T(8,128)(2,1)} %k_ref.1, bf16[128,512]{1,0:T(8,128)(2,1)} %v_ref.1, bf16[128,512]{1,0:T(8,128)(2,1)} %o_ref.1, bf16[128,512]{1,0:T(8,128)(2,1)} %g_ref.1, f32[4,128]{1,0:T(4,128)} %bitcast.3), custom_call_target="tpu_custom_call" | custom-call | tf_op jit(solution)/shard_map/pallas_call | solution.py:268
  3.2 26.2 %all_to_all.20.in_ref = bf16[16,136,128]{2,1,0:T(8,128)(2,1)S(1)} all-to-all(bf16[16,136,128]{2,1,0:T(8,128)(2,1)} %shard_map.94), channel_id=1, replica_groups=mesh['qrow'=16,'kcol_h'=4,'kcol_s'=4] {'kcol_h','kcol_s'}, dimensions={0} | all-to-all | bytes 1114112 | tf_op jit(solution)/shard_map/all_to_all | solution.py:275
  29.4 1.3 %shard_map.95 = (bf16[16,5,64,128]{3,2,1,0:T(8,128)(2,1)}, bf16[16,64,128]{2,1,0:T(8,128)(2,1)S(1)}) custom-call(bf16[16,136,128]{2,1,0:T(8,128)(2,1)S(1)} %all_to_all.20.in_ref), custom_call_target="tpu_custom_call" | custom-call | tf_op jit(solution)/shard_map/pallas_call | solution.py:276
  30.6 0.0 copy-start
  30.6 6.3 %all-to-all-start.1 = ((bf16[16,5,64,128]{3,2,1,0:T(8,128)(2,1)}), bf16[16,5,64,128]{3,2,1,0:T(8,128)(2,1)S(1)}, u32[]{:S(2)}, u32[]{:S(2)}) async-start(bf16[16,5,64,128]{3,2,1,0:T(8,128)(2,1)} %get-tuple-element.13), calls=%async_computation.1 | async-start | bytes 2621440 | tf_op jit(solution)/shard_map/all_to_all | solution.py:283
  36.9 0.7 collective-permute-start.2
  37.6 1.4 %collective-permute-start = (bf16[16,64,128]{2,1,0:T(8,128)(2,1)S(1)}, bf16[16,64,128]{2,1,0:T(8,128)(2,1)S(1)}, u32[]{:S(2)}, u32[]{:S(2)}) collective-permute-start(bf16[16,64,128]{2,1,0:T(8,128)(2,1)S(1)} %get-tuple-element.12.qg0), channel_id=1, source_target_pairs={{0,1},{1,0},{2,3},{3,2},{4,5},{5,4},{6,7},{7,6},{8,9},{9,8},{10,11... | collective-permute-start | bytes 786440 | tf_op jit(solution)/shard_map/ppermute | solution.py:237
  39.1 10.3 %collective-permute-done.2.qg2 = bf16[16,64,128]{2,1,0:T(8,128)(2,1)S(1)} collective-permute-done((bf16[16,64,128]{2,1,0:T(8,128)(2,1)S(1)}, bf16[16,64,128]{2,1,0:T(8,128)(2,1)S(1)}, u32[]{:S(2)}, u32[]{:S(2)}) %collective-permute-start.2) | collective-permute-done | bytes 262176 | tf_op jit(solution)/shard_map/ppermute | solution.py:237
  49.3 4.1 %collective-permute-start.3 = (bf16[16,64,128]{2,1,0:T(8,128)(2,1)S(1)}, bf16[16,64,128]{2,1,0:T(8,128)(2,1)S(1)}, u32[]{:S(2)}, u32[]{:S(2)}) collective-permute-start(bf16[16,64,128]{2,1,0:T(8,128)(2,1)S(1)} %collective-permute-done.2.qg2), channel_id=1, source_target_pairs={{0,1},{1,0},{2,3},{3,2},{4,5},{5,4},{6,7},{7,6},{8,9},{9,8},{10,11... | collective-permute-start | bytes 786440 | tf_op jit(solution)/shard_map/ppermute | solution.py:237
  53.4 0.1 pad_add_fusion.place_ref
  53.5 0.0 collective-permute-done.qg1
  53.5 4.2 %all-to-all-done.1.kv_ref = bf16[16,5,64,128]{3,2,1,0:T(8,128)(2,1)S(1)} async-done(((bf16[16,5,64,128]{3,2,1,0:T(8,128)(2,1)}), bf16[16,5,64,128]{3,2,1,0:T(8,128)(2,1)S(1)}, u32[]{:S(2)}, u32[]{:S(2)}) %all-to-all-start.1) | async-done | bytes 1310752 | tf_op jit(solution)/shard_map/all_to_all | solution.py:283
  57.7 0.0 copy-done
  57.7 2.9 %shard_map.96 = (bf16[16,32,128]{2,1,0:T(8,128)(2,1)S(1)}, bf16[16,32,128]{2,1,0:T(8,128)(2,1)S(1)}, f32[5,512,128]{2,1,0:T(8,128)S(1)}, f32[5,512,128]{2,1,0:T(8,128)S(1)}) custom-call(s32[2]{0:T(128)S(1)} %pad_add_fusion.place_ref, s32[8]{0:T(128)S(1)} %copy-done, bf16[16,136,128]{2,1,0:T(8,128)(2,1)S(1)} %all_to_all.20.in_ref, ...), custom_call_target="tpu_custom_call" | custom-call | tf_op jit(solution)/shard_map/pallas_call | solution.py:245
  60.6 0.0 collective-permute-done.3.qg3
  60.6 4.2 %shard_map.97 = (bf16[16,32,128]{2,1,0:T(8,128)(2,1)S(1)}, bf16[16,32,128]{2,1,0:T(8,128)(2,1)S(1)}, bf16[16,5,64,128]{3,2,1,0:T(8,128)(2,1)}) custom-call(s32[2]{0:T(128)S(1)} %pad_add_fusion.place_ref, s32[8]{0:T(128)S(1)} %copy-done, bf16[16,136,128]{2,1,0:T(8,128)(2,1)S(1)} %all_to_all.20.in_ref, bf16[16,64,128]{2,1,0:T(8,128)(2,1)S(1)} %collective-permute-done.2.qg2, ...), custom_call_target="tpu_custom_call" | custom-call | tf_op jit(solution)/shard_map/pallas_call | solution.py:253
  64.9 11.8 %all-to-all-start.2 = ((bf16[16,5,64,128]{3,2,1,0:T(8,128)(2,1)}), bf16[16,5,64,128]{3,2,1,0:T(8,128)(2,1)S(1)}, u32[]{:S(2)}, u32[]{:S(2)}) async-start(bf16[16,5,64,128]{3,2,1,0:T(8,128)(2,1)} %get-tuple-element.20), calls=%async_computation.2 | async-start | bytes 2621440 | tf_op jit(solution)/shard_map/all_to_all | solution.py:287
  76.6 1.4 %collective-permute-start.1 = (bf16[16,32,128]{2,1,0:T(8,128)(2,1)S(1)}, bf16[16,32,128]{2,1,0:T(8,128)(2,1)S(1)}, u32[]{:S(2)}, u32[]{:S(2)}) collective-permute-start(bf16[16,32,128]{2,1,0:T(8,128)(2,1)S(1)} %get-tuple-element.15), channel_id=1, source_target_pairs={{0,1},{1,0},{2,3},{3,2},{4,5},{5,4},{6,7},{7,6},{8,9},{9,8},{10,11... | collective-permute-start | bytes 393224 | tf_op jit(solution)/shard_map/ppermute | solution.py:237
  78.1 0.7 collective-permute-start.4
  78.8 1.4 %collective-permute-start.5 = (bf16[16,32,128]{2,1,0:T(8,128)(2,1)S(1)}, bf16[16,32,128]{2,1,0:T(8,128)(2,1)S(1)}, u32[]{:S(2)}, u32[]{:S(2)}) collective-permute-start(bf16[16,32,128]{2,1,0:T(8,128)(2,1)S(1)} %get-tuple-element.19), channel_id=1, source_target_pairs={{0,3},{1,2},{2,1},{3,0},{4,7},{5,6},{6,5},{7,4},{8,11},{9,10},{10,... | collective-permute-start | bytes 393224 | tf_op jit(solution)/shard_map/ppermute | solution.py:237
  80.2 2.8 %collective-permute-done.1.dq1 = bf16[16,32,128]{2,1,0:T(8,128)(2,1)S(1)} collective-permute-done((bf16[16,32,128]{2,1,0:T(8,128)(2,1)S(1)}, bf16[16,32,128]{2,1,0:T(8,128)(2,1)S(1)}, u32[]{:S(2)}, u32[]{:S(2)}) %collective-permute-start.1) | collective-permute-done | bytes 131104 | tf_op jit(solution)/shard_map/ppermute | solution.py:237
  83.0 5.3 %collective-permute-done.4.dq2 = bf16[16,32,128]{2,1,0:T(8,128)(2,1)S(1)} collective-permute-done((bf16[16,32,128]{2,1,0:T(8,128)(2,1)S(1)}, bf16[16,32,128]{2,1,0:T(8,128)(2,1)S(1)}, u32[]{:S(2)}, u32[]{:S(2)}) %collective-permute-start.4) | collective-permute-done | bytes 131104 | tf_op jit(solution)/shard_map/ppermute | solution.py:237
  88.3 3.8 %collective-permute-done.5.dq3 = bf16[16,32,128]{2,1,0:T(8,128)(2,1)S(1)} collective-permute-done((bf16[16,32,128]{2,1,0:T(8,128)(2,1)S(1)}, bf16[16,32,128]{2,1,0:T(8,128)(2,1)S(1)}, u32[]{:S(2)}, u32[]{:S(2)}) %collective-permute-start.5) | collective-permute-done | bytes 131104 | tf_op jit(solution)/shard_map/ppermute | solution.py:237
  92.1 5.3 %all-to-all-done.2.dkv_ref = bf16[16,5,64,128]{3,2,1,0:T(8,128)(2,1)S(1)} async-done(((bf16[16,5,64,128]{3,2,1,0:T(8,128)(2,1)}), bf16[16,5,64,128]{3,2,1,0:T(8,128)(2,1)S(1)}, u32[]{:S(2)}, u32[]{:S(2)}) %all-to-all-start.2) | async-done | bytes 1310752 | tf_op jit(solution)/shard_map/all_to_all | solution.py:287
  97.4 0.2 shard_map.98
  97.6 17.9 %all_to_all.21.in_ref = bf16[16,96,128]{2,1,0:T(8,128)(2,1)S(1)} all-to-all(bf16[16,96,128]{2,1,0:T(8,128)(2,1)S(1)} %shard_map.98), channel_id=1, replica_groups=mesh['qrow'=16,'kcol_h'=4,'kcol_s'=4] {'kcol_h','kcol_s'}, dimensions={0} | all-to-all | bytes 786432 | tf_op jit(solution)/shard_map/all_to_all | solution.py:296
  115.6 0.8 shard_map.99
Async XLA Ops:
  30.6 27.1 %copy-start = (s32[8]{0:T(128)S(1)}, s32[8]{0:T(128)}, u32[]{:S(2)}) copy-start(s32[8]{0:T(128)} %lengths_ref.3) | copy-start | bytes 100
  30.6 27.1 %all-to-all-start.1 = ((bf16[16,5,64,128]{3,2,1,0:T(8,128)(2,1)}), bf16[16,5,64,128]{3,2,1,0:T(8,128)(2,1)S(1)}, u32[]{:S(2)}, u32[]{:S(2)}) async-start(bf16[16,5,64,128]{3,2,1,0:T(8,128)(2,1)} %get-tuple-element.13), calls=%async_computation.1 | async-start | bytes 2621440 | tf_op jit(solution)/shard_map/all_to_all | solution.py:283
  36.9 12.4 %collective-permute-start.2 = (bf16[16,64,128]{2,1,0:T(8,128)(2,1)S(1)}, bf16[16,64,128]{2,1,0:T(8,128)(2,1)S(1)}, u32[]{:S(2)}, u32[]{:S(2)}) collective-permute-start(bf16[16,64,128]{2,1,0:T(8,128)(2,1)S(1)} %get-tuple-element.12.qg0), channel_id=1, source_target_pairs={{0,2},{1,3},{2,0},{3,1},{4,6},{5,7},{6,4},{7,5},{8,10},{9,11},{10,... | collective-permute-start | bytes 786440 | tf_op jit(solution)/shard_map/ppermute | solution.py:237
  37.6 15.9 %collective-permute-start = (bf16[16,64,128]{2,1,0:T(8,128)(2,1)S(1)}, bf16[16,64,128]{2,1,0:T(8,128)(2,1)S(1)}, u32[]{:S(2)}, u32[]{:S(2)}) collective-permute-start(bf16[16,64,128]{2,1,0:T(8,128)(2,1)S(1)} %get-tuple-element.12.qg0), channel_id=1, source_target_pairs={{0,1},{1,0},{2,3},{3,2},{4,5},{5,4},{6,7},{7,6},{8,9},{9,8},{10,11... | collective-permute-start | bytes 786440 | tf_op jit(solution)/shard_map/ppermute | solution.py:237
  49.3 11.3 %collective-permute-start.3 = (bf16[16,64,128]{2,1,0:T(8,128)(2,1)S(1)}, bf16[16,64,128]{2,1,0:T(8,128)(2,1)S(1)}, u32[]{:S(2)}, u32[]{:S(2)}) collective-permute-start(bf16[16,64,128]{2,1,0:T(8,128)(2,1)S(1)} %collective-permute-done.2.qg2), channel_id=1, source_target_pairs={{0,1},{1,0},{2,3},{3,2},{4,5},{5,4},{6,7},{7,6},{8,9},{9,8},{10,11... | collective-permute-start | bytes 786440 | tf_op jit(solution)/shard_map/ppermute | solution.py:237
  64.9 32.6 %all-to-all-start.2 = ((bf16[16,5,64,128]{3,2,1,0:T(8,128)(2,1)}), bf16[16,5,64,128]{3,2,1,0:T(8,128)(2,1)S(1)}, u32[]{:S(2)}, u32[]{:S(2)}) async-start(bf16[16,5,64,128]{3,2,1,0:T(8,128)(2,1)} %get-tuple-element.20), calls=%async_computation.2 | async-start | bytes 2621440 | tf_op jit(solution)/shard_map/all_to_all | solution.py:287
  76.6 6.4 %collective-permute-start.1 = (bf16[16,32,128]{2,1,0:T(8,128)(2,1)S(1)}, bf16[16,32,128]{2,1,0:T(8,128)(2,1)S(1)}, u32[]{:S(2)}, u32[]{:S(2)}) collective-permute-start(bf16[16,32,128]{2,1,0:T(8,128)(2,1)S(1)} %get-tuple-element.15), channel_id=1, source_target_pairs={{0,1},{1,0},{2,3},{3,2},{4,5},{5,4},{6,7},{7,6},{8,9},{9,8},{10,11... | collective-permute-start | bytes 393224 | tf_op jit(solution)/shard_map/ppermute | solution.py:237
  78.1 10.2 %collective-permute-start.4 = (bf16[16,32,128]{2,1,0:T(8,128)(2,1)S(1)}, bf16[16,32,128]{2,1,0:T(8,128)(2,1)S(1)}, u32[]{:S(2)}, u32[]{:S(2)}) collective-permute-start(bf16[16,32,128]{2,1,0:T(8,128)(2,1)S(1)} %get-tuple-element.18), channel_id=1, source_target_pairs={{0,2},{1,3},{2,0},{3,1},{4,6},{5,7},{6,4},{7,5},{8,10},{9,11},{10,... | collective-permute-start | bytes 393224 | tf_op jit(solution)/shard_map/ppermute | solution.py:237
  78.8 13.3 %collective-permute-start.5 = (bf16[16,32,128]{2,1,0:T(8,128)(2,1)S(1)}, bf16[16,32,128]{2,1,0:T(8,128)(2,1)S(1)}, u32[]{:S(2)}, u32[]{:S(2)}) collective-permute-start(bf16[16,32,128]{2,1,0:T(8,128)(2,1)S(1)} %get-tuple-element.19), channel_id=1, source_target_pairs={{0,3},{1,2},{2,1},{3,0},{4,7},{5,6},{6,5},{7,4},{8,11},{9,10},{10,... | collective-permute-start | bytes 393224 | tf_op jit(solution)/shard_map/ppermute | solution.py:237

commit v5 on v4

--- a/solution.py
+++ b/solution.py
@@ -95,8 +95,6 @@
     for i, ref in enumerate(qg_refs):
         q_all[:, i] = ref[:, 0:STRIP]
         g_all[:, i] = ref[:, STRIP : 2 * STRIP]
-    dk_acc[...] = jnp.zeros_like(dk_acc)
-    dv_acc[...] = jnp.zeros_like(dv_acc)
     j_tile = KROWS // STRIP
     per_block = BLOCK // KSPAN
     k_iota = lax.broadcasted_iota(jnp.int32, (KROWS, 1), 0)
@@ -186,6 +184,8 @@
     place_ref, lengths_ref, in_ref, qg0, qg1, kv_ref,
     dq0, dq1, dk_acc, dv_acc, dq_acc, q_all, g_all,
 ):
+    dk_acc[...] = jnp.zeros_like(dk_acc)
+    dv_acc[...] = jnp.zeros_like(dv_acc)
     tiles(0, place_ref, lengths_ref, in_ref, (qg0, qg1), kv_ref, (dq0, dq1), dk_acc, dv_acc, dq_acc, q_all, g_all)
 
 
@@ -193,14 +193,16 @@
     place_ref, lengths_ref, in_ref, qg2, qg3, kv_ref, dk_in, dv_in,
     dq2, dq3, dkv_ref, dk_acc, dv_acc, dq_acc, q_all, g_all,
 ):
+    dk_acc[...] = dk_in[...]
+    dv_acc[...] = dv_in[...]
     tiles(1, place_ref, lengths_ref, in_ref, (qg2, qg3), kv_ref, (dq2, dq3), dk_acc, dv_acc, dq_acc, q_all, g_all)
     j_tile = KROWS // STRIP
     per_block = BLOCK // KSPAN
     for kt in range(REACH * per_block):
         js = slice((kt % per_block) * j_tile, (kt % per_block + 1) * j_tile)
         back = REACH - 1 - kt // per_block
-        dk = (dk_acc[kt] + dk_in[kt]) * SCALE
-        dv = dv_acc[kt] + dv_in[kt]
+        dk = dk_acc[kt] * SCALE
+        dv = dv_acc[kt]
         dkv_ref[js, back, 0:STRIP] = dk.astype(BF16).reshape(j_tile, STRIP, HEAD_DIM)
         dkv_ref[js, back, STRIP : 2 * STRIP] = dv.astype(BF16).reshape(j_tile, STRIP, HEAD_DIM)
 

time: 117 us -> 120 us (1.026)
  starting transfers between devices: 27.8 us -> 32 us
    all_to_all x1, starting transfers between devices: 11.8 us -> 16 us  [per_device(): dkv = lax.all_to_all(dkv_part, 'qrow', 0, 0)]
where the time goes in v5:
time: 120 us
  blocking collectives  44.1 us (37%)
  starting transfers between devices  32 us (27%)
  waiting for transfers between devices  31.7 us (26%)
  Pallas kernels  11.8 us (10%)
    all_to_all x1, blocking collectives, per_device(): mine = lax.all_to_all(packed, KCOL, 0, 0)  26.2 us
    ppermute x6, waiting for transfers between devices, from_partner(): return lax.ppermute(x, STRIPS, [(d, d ^ s) for d in range(WAYS)])  22.2 us
    all_to_all x1, blocking collectives, per_device(): back = lax.all_to_all(sums, KCOL, 0, 0)  17.9 us
    all_to_all x1, starting transfers between devices, per_device(): dkv = lax.all_to_all(dkv_part, 'qrow', 0, 0)  16 us
    ppermute x6, starting transfers between devices, from_partner(): return lax.ppermute(x, STRIPS, [(d, d ^ s) for d in range(WAYS)])  9.78 us
    all_to_all x1, starting transfers between devices, per_device(): keys = lax.all_to_all(spread, 'qrow', 0, 0)  6.27 us
    all_to_all x1, waiting for transfers between devices, per_device(): dkv = lax.all_to_all(dkv_part, 'qrow', 0, 0)  5.32 us
    all_to_all x1, waiting for transfers between devices, per_device(): keys = lax.all_to_all(spread, 'qrow', 0, 0)  4.23 us
  transfers between devices with their start and end apart: 8, of which 6 were waited for; matrix products, arithmetic and copies ran while one was open for 0% of the time, Pallas kernels for 2%

profile of v5, /device:TPU:40, one launch (start us, length us, event | category | flops | bytes accessed | tf_op | source)
XLA Modules:
  0.0 120.4 jit_solution(7932862447693934731)
XLA Ops:
  0.6 2.6 %shard_map.94 = bf16[16,136,128]{2,1,0:T(8,128)(2,1)} custom-call(bf16[128,512]{1,0:T(8,128)(2,1)} %q_ref.1, bf16[128,512]{1,0:T(8,128)(2,1)} %k_ref.1, bf16[128,512]{1,0:T(8,128)(2,1)} %v_ref.1, bf16[128,512]{1,0:T(8,128)(2,1)} %o_ref.1, bf16[128,512]{1,0:T(8,128)(2,1)} %g_ref.1, f32[4,128]{1,0:T(4,128)} %bitcast.3), custom_call_target="tpu_custom_call" | custom-call | tf_op jit(solution)/shard_map/pallas_call | solution.py:270
  3.2 26.2 %all_to_all.20.in_ref = bf16[16,136,128]{2,1,0:T(8,128)(2,1)S(1)} all-to-all(bf16[16,136,128]{2,1,0:T(8,128)(2,1)} %shard_map.94), channel_id=1, replica_groups=mesh['qrow'=16,'kcol_h'=4,'kcol_s'=4] {'kcol_h','kcol_s'}, dimensions={0} | all-to-all | bytes 1114112 | tf_op jit(solution)/shard_map/all_to_all | solution.py:277
  29.4 1.3 %shard_map.95 = (bf16[16,5,64,128]{3,2,1,0:T(8,128)(2,1)}, bf16[16,64,128]{2,1,0:T(8,128)(2,1)S(1)}) custom-call(bf16[16,136,128]{2,1,0:T(8,128)(2,1)S(1)} %all_to_all.20.in_ref), custom_call_target="tpu_custom_call" | custom-call | tf_op jit(solution)/shard_map/pallas_call | solution.py:278
  30.6 0.0 copy-start
  30.6 6.3 %all-to-all-start.1 = ((bf16[16,5,64,128]{3,2,1,0:T(8,128)(2,1)}), bf16[16,5,64,128]{3,2,1,0:T(8,128)(2,1)S(1)}, u32[]{:S(2)}, u32[]{:S(2)}) async-start(bf16[16,5,64,128]{3,2,1,0:T(8,128)(2,1)} %get-tuple-element.13), calls=%async_computation.1 | async-start | bytes 2621440 | tf_op jit(solution)/shard_map/all_to_all | solution.py:285
  36.9 0.7 collective-permute-start.2
  37.6 1.4 %collective-permute-start = (bf16[16,64,128]{2,1,0:T(8,128)(2,1)S(1)}, bf16[16,64,128]{2,1,0:T(8,128)(2,1)S(1)}, u32[]{:S(2)}, u32[]{:S(2)}) collective-permute-start(bf16[16,64,128]{2,1,0:T(8,128)(2,1)S(1)} %get-tuple-element.12.qg0), channel_id=1, source_target_pairs={{0,1},{1,0},{2,3},{3,2},{4,5},{5,4},{6,7},{7,6},{8,9},{9,8},{10,11... | collective-permute-start | bytes 786440 | tf_op jit(solution)/shard_map/ppermute | solution.py:239
  39.1 10.3 %collective-permute-done.2.qg2 = bf16[16,64,128]{2,1,0:T(8,128)(2,1)S(1)} collective-permute-done((bf16[16,64,128]{2,1,0:T(8,128)(2,1)S(1)}, bf16[16,64,128]{2,1,0:T(8,128)(2,1)S(1)}, u32[]{:S(2)}, u32[]{:S(2)}) %collective-permute-start.2) | collective-permute-done | bytes 262176 | tf_op jit(solution)/shard_map/ppermute | solution.py:239
  49.3 4.1 %collective-permute-start.3 = (bf16[16,64,128]{2,1,0:T(8,128)(2,1)S(1)}, bf16[16,64,128]{2,1,0:T(8,128)(2,1)S(1)}, u32[]{:S(2)}, u32[]{:S(2)}) collective-permute-start(bf16[16,64,128]{2,1,0:T(8,128)(2,1)S(1)} %collective-permute-done.2.qg2), channel_id=1, source_target_pairs={{0,1},{1,0},{2,3},{3,2},{4,5},{5,4},{6,7},{7,6},{8,9},{9,8},{10,11... | collective-permute-start | bytes 786440 | tf_op jit(solution)/shard_map/ppermute | solution.py:239
  53.4 0.1 pad_add_fusion.place_ref
  53.5 0.0 collective-permute-done.qg1
  53.5 4.2 %all-to-all-done.1.kv_ref = bf16[16,5,64,128]{3,2,1,0:T(8,128)(2,1)S(1)} async-done(((bf16[16,5,64,128]{3,2,1,0:T(8,128)(2,1)}), bf16[16,5,64,128]{3,2,1,0:T(8,128)(2,1)S(1)}, u32[]{:S(2)}, u32[]{:S(2)}) %all-to-all-start.1) | async-done | bytes 1310752 | tf_op jit(solution)/shard_map/all_to_all | solution.py:285
  57.7 0.0 copy-done
  57.7 2.9 %shard_map.96 = (bf16[16,32,128]{2,1,0:T(8,128)(2,1)S(1)}, bf16[16,32,128]{2,1,0:T(8,128)(2,1)S(1)}, f32[5,512,128]{2,1,0:T(8,128)S(1)}, f32[5,512,128]{2,1,0:T(8,128)S(1)}) custom-call(s32[2]{0:T(128)S(1)} %pad_add_fusion.place_ref, s32[8]{0:T(128)S(1)} %copy-done, bf16[16,136,128]{2,1,0:T(8,128)(2,1)S(1)} %all_to_all.20.in_ref, ...), custom_call_target="tpu_custom_call" | custom-call | tf_op jit(solution)/shard_map/pallas_call | solution.py:247
  60.6 0.0 collective-permute-done.3.qg3
  60.6 4.0 %shard_map.97 = (bf16[16,32,128]{2,1,0:T(8,128)(2,1)S(1)}, bf16[16,32,128]{2,1,0:T(8,128)(2,1)S(1)}, bf16[16,5,64,128]{3,2,1,0:T(8,128)(2,1)}) custom-call(s32[2]{0:T(128)S(1)} %pad_add_fusion.place_ref, s32[8]{0:T(128)S(1)} %copy-done, bf16[16,136,128]{2,1,0:T(8,128)(2,1)S(1)} %all_to_all.20.in_ref, bf16[16,64,128]{2,1,0:T(8,128)(2,1)S(1)} %collective-permute-done.2.qg2, ...), custom_call_target="tpu_custom_call" | custom-call | tf_op jit(solution)/shard_map/pallas_call | solution.py:255
  64.7 16.0 %all-to-all-start.2 = ((bf16[16,5,64,128]{3,2,1,0:T(8,128)(2,1)}), bf16[16,5,64,128]{3,2,1,0:T(8,128)(2,1)S(1)}, u32[]{:S(2)}, u32[]{:S(2)}) async-start(bf16[16,5,64,128]{3,2,1,0:T(8,128)(2,1)} %get-tuple-element.20), calls=%async_computation.2 | async-start | bytes 2621440 | tf_op jit(solution)/shard_map/all_to_all | solution.py:289
  80.7 1.4 %collective-permute-start.1 = (bf16[16,32,128]{2,1,0:T(8,128)(2,1)S(1)}, bf16[16,32,128]{2,1,0:T(8,128)(2,1)S(1)}, u32[]{:S(2)}, u32[]{:S(2)}) collective-permute-start(bf16[16,32,128]{2,1,0:T(8,128)(2,1)S(1)} %get-tuple-element.15), channel_id=1, source_target_pairs={{0,1},{1,0},{2,3},{3,2},{4,5},{5,4},{6,7},{7,6},{8,9},{9,8},{10,11... | collective-permute-start | bytes 393224 | tf_op jit(solution)/shard_map/ppermute | solution.py:239
  82.1 0.7 collective-permute-start.4
  82.8 1.4 %collective-permute-start.5 = (bf16[16,32,128]{2,1,0:T(8,128)(2,1)S(1)}, bf16[16,32,128]{2,1,0:T(8,128)(2,1)S(1)}, u32[]{:S(2)}, u32[]{:S(2)}) collective-permute-start(bf16[16,32,128]{2,1,0:T(8,128)(2,1)S(1)} %get-tuple-element.19), channel_id=1, source_target_pairs={{0,3},{1,2},{2,1},{3,0},{4,7},{5,6},{6,5},{7,4},{8,11},{9,10},{10,... | collective-permute-start | bytes 393224 | tf_op jit(solution)/shard_map/ppermute | solution.py:239
  84.2 2.8 %collective-permute-done.1.dq1 = bf16[16,32,128]{2,1,0:T(8,128)(2,1)S(1)} collective-permute-done((bf16[16,32,128]{2,1,0:T(8,128)(2,1)S(1)}, bf16[16,32,128]{2,1,0:T(8,128)(2,1)S(1)}, u32[]{:S(2)}, u32[]{:S(2)}) %collective-permute-start.1) | collective-permute-done | bytes 131104 | tf_op jit(solution)/shard_map/ppermute | solution.py:239
  87.1 5.3 %collective-permute-done.4.dq2 = bf16[16,32,128]{2,1,0:T(8,128)(2,1)S(1)} collective-permute-done((bf16[16,32,128]{2,1,0:T(8,128)(2,1)S(1)}, bf16[16,32,128]{2,1,0:T(8,128)(2,1)S(1)}, u32[]{:S(2)}, u32[]{:S(2)}) %collective-permute-start.4) | collective-permute-done | bytes 131104 | tf_op jit(solution)/shard_map/ppermute | solution.py:239
  92.3 3.8 %collective-permute-done.5.dq3 = bf16[16,32,128]{2,1,0:T(8,128)(2,1)S(1)} collective-permute-done((bf16[16,32,128]{2,1,0:T(8,128)(2,1)S(1)}, bf16[16,32,128]{2,1,0:T(8,128)(2,1)S(1)}, u32[]{:S(2)}, u32[]{:S(2)}) %collective-permute-start.5) | collective-permute-done | bytes 131104 | tf_op jit(solution)/shard_map/ppermute | solution.py:239
  96.1 5.3 %all-to-all-done.2.dkv_ref = bf16[16,5,64,128]{3,2,1,0:T(8,128)(2,1)S(1)} async-done(((bf16[16,5,64,128]{3,2,1,0:T(8,128)(2,1)}), bf16[16,5,64,128]{3,2,1,0:T(8,128)(2,1)S(1)}, u32[]{:S(2)}, u32[]{:S(2)}) %all-to-all-start.2) | async-done | bytes 1310752 | tf_op jit(solution)/shard_map/all_to_all | solution.py:289
  101.4 0.2 shard_map.98
  101.7 17.9 %all_to_all.21.in_ref = bf16[16,96,128]{2,1,0:T(8,128)(2,1)S(1)} all-to-all(bf16[16,96,128]{2,1,0:T(8,128)(2,1)S(1)} %shard_map.98), channel_id=1, replica_groups=mesh['qrow'=16,'kcol_h'=4,'kcol_s'=4] {'kcol_h','kcol_s'}, dimensions={0} | all-to-all | bytes 786432 | tf_op jit(solution)/shard_map/all_to_all | solution.py:298
  119.6 0.8 shard_map.99
Async XLA Ops:
  30.6 27.1 %copy-start = (s32[8]{0:T(128)S(1)}, s32[8]{0:T(128)}, u32[]{:S(2)}) copy-start(s32[8]{0:T(128)} %lengths_ref.3) | copy-start | bytes 100
  30.6 27.1 %all-to-all-start.1 = ((bf16[16,5,64,128]{3,2,1,0:T(8,128)(2,1)}), bf16[16,5,64,128]{3,2,1,0:T(8,128)(2,1)S(1)}, u32[]{:S(2)}, u32[]{:S(2)}) async-start(bf16[16,5,64,128]{3,2,1,0:T(8,128)(2,1)} %get-tuple-element.13), calls=%async_computation.1 | async-start | bytes 2621440 | tf_op jit(solution)/shard_map/all_to_all | solution.py:285
  36.9 12.4 %collective-permute-start.2 = (bf16[16,64,128]{2,1,0:T(8,128)(2,1)S(1)}, bf16[16,64,128]{2,1,0:T(8,128)(2,1)S(1)}, u32[]{:S(2)}, u32[]{:S(2)}) collective-permute-start(bf16[16,64,128]{2,1,0:T(8,128)(2,1)S(1)} %get-tuple-element.12.qg0), channel_id=1, source_target_pairs={{0,2},{1,3},{2,0},{3,1},{4,6},{5,7},{6,4},{7,5},{8,10},{9,11},{10,... | collective-permute-start | bytes 786440 | tf_op jit(solution)/shard_map/ppermute | solution.py:239
  37.6 15.9 %collective-permute-start = (bf16[16,64,128]{2,1,0:T(8,128)(2,1)S(1)}, bf16[16,64,128]{2,1,0:T(8,128)(2,1)S(1)}, u32[]{:S(2)}, u32[]{:S(2)}) collective-permute-start(bf16[16,64,128]{2,1,0:T(8,128)(2,1)S(1)} %get-tuple-element.12.qg0), channel_id=1, source_target_pairs={{0,1},{1,0},{2,3},{3,2},{4,5},{5,4},{6,7},{7,6},{8,9},{9,8},{10,11... | collective-permute-start | bytes 786440 | tf_op jit(solution)/shard_map/ppermute | solution.py:239
  49.3 11.3 %collective-permute-start.3 = (bf16[16,64,128]{2,1,0:T(8,128)(2,1)S(1)}, bf16[16,64,128]{2,1,0:T(8,128)(2,1)S(1)}, u32[]{:S(2)}, u32[]{:S(2)}) collective-permute-start(bf16[16,64,128]{2,1,0:T(8,128)(2,1)S(1)} %collective-permute-done.2.qg2), channel_id=1, source_target_pairs={{0,1},{1,0},{2,3},{3,2},{4,5},{5,4},{6,7},{7,6},{8,9},{9,8},{10,11... | collective-permute-start | bytes 786440 | tf_op jit(solution)/shard_map/ppermute | solution.py:239
  64.7 36.8 %all-to-all-start.2 = ((bf16[16,5,64,128]{3,2,1,0:T(8,128)(2,1)}), bf16[16,5,64,128]{3,2,1,0:T(8,128)(2,1)S(1)}, u32[]{:S(2)}, u32[]{:S(2)}) async-start(bf16[16,5,64,128]{3,2,1,0:T(8,128)(2,1)} %get-tuple-element.20), calls=%async_computation.2 | async-start | bytes 2621440 | tf_op jit(solution)/shard_map/all_to_all | solution.py:289
  80.7 6.4 %collective-permute-start.1 = (bf16[16,32,128]{2,1,0:T(8,128)(2,1)S(1)}, bf16[16,32,128]{2,1,0:T(8,128)(2,1)S(1)}, u32[]{:S(2)}, u32[]{:S(2)}) collective-permute-start(bf16[16,32,128]{2,1,0:T(8,128)(2,1)S(1)} %get-tuple-element.15), channel_id=1, source_target_pairs={{0,1},{1,0},{2,3},{3,2},{4,5},{5,4},{6,7},{7,6},{8,9},{9,8},{10,11... | collective-permute-start | bytes 393224 | tf_op jit(solution)/shard_map/ppermute | solution.py:239
  82.1 10.2 %collective-permute-start.4 = (bf16[16,32,128]{2,1,0:T(8,128)(2,1)S(1)}, bf16[16,32,128]{2,1,0:T(8,128)(2,1)S(1)}, u32[]{:S(2)}, u32[]{:S(2)}) collective-permute-start(bf16[16,32,128]{2,1,0:T(8,128)(2,1)S(1)} %get-tuple-element.18), channel_id=1, source_target_pairs={{0,2},{1,3},{2,0},{3,1},{4,6},{5,7},{6,4},{7,5},{8,10},{9,11},{10,... | collective-permute-start | bytes 393224 | tf_op jit(solution)/shard_map/ppermute | solution.py:239
  82.8 13.3 %collective-permute-start.5 = (bf16[16,32,128]{2,1,0:T(8,128)(2,1)S(1)}, bf16[16,32,128]{2,1,0:T(8,128)(2,1)S(1)}, u32[]{:S(2)}, u32[]{:S(2)}) collective-permute-start(bf16[16,32,128]{2,1,0:T(8,128)(2,1)S(1)} %get-tuple-element.19), channel_id=1, source_target_pairs={{0,3},{1,2},{2,1},{3,0},{4,7},{5,6},{6,5},{7,4},{8,11},{9,10},{10,... | collective-permute-start | bytes 393224 | tf_op jit(solution)/shard_map/ppermute | solution.py:239

commit v6 on v5

--- a/solution.py
+++ b/solution.py
@@ -127,7 +127,6 @@
         doc_last = jnp.where(end <= last, end, doc_last)
         q_doc = jnp.where(end <= q_pos, end, q_doc)
     low = (doc_first - base) // KSPAN
-    high = (last - base) // KSPAN
     q = q_all[ms].reshape(QROWS, HEAD_DIM)
     g = g_all[ms].reshape(QROWS, HEAD_DIM)
 
@@ -140,22 +139,22 @@
 
     norm, delta = row(0), row(3)
 
-    def one_tile(kt, masked):
-        js = pl.ds((kt % per_block) * j_tile, j_tile)
+    def one_tile(kt, masked, rows=KROWS):
+        js = pl.ds((kt % per_block) * j_tile, rows // STRIP)
         back = REACH - 1 - kt // per_block
-        k = kv_ref[js, back, 0:STRIP].reshape(KROWS, HEAD_DIM)
-        v = kv_ref[js, back, STRIP : 2 * STRIP].reshape(KROWS, HEAD_DIM)
+        k = kv_ref[js, back, 0:STRIP].reshape(rows, HEAD_DIM)
+        v = kv_ref[js, back, STRIP : 2 * STRIP].reshape(rows, HEAD_DIM)
         across = (((1,), (1,)), ((), ()))
         s = lax.dot_general(k, q, across, preferred_element_type=F32)
         p = jnp.exp2(s * (SCALE * LOG2E) - norm)
         if masked:
-            k_pos = k_iota + (base + kt * KSPAN)
+            k_pos = k_iota[:rows] + (base + kt * KSPAN)
             p = jnp.where((k_pos <= q_pos) & (k_pos >= q_doc), p, 0.0)
         dp = lax.dot_general(v, g, across, preferred_element_type=F32)
         ds = (p * (dp - delta)).astype(BF16)
         p = p.astype(BF16)
-        dv_acc[kt] += jnp.dot(p, g, preferred_element_type=F32)
-        dk_acc[kt] += jnp.dot(ds, q, preferred_element_type=F32)
+        dv_acc[kt, 0:rows] += jnp.dot(p, g, preferred_element_type=F32)
+        dk_acc[kt, 0:rows] += jnp.dot(ds, q, preferred_element_type=F32)
         dq_acc[...] += lax.dot_general(
             k, ds, (((0,), (0,)), ((), ())), preferred_element_type=F32
         )
@@ -174,7 +173,9 @@
 
         return carry
 
-    lax.fori_loop(low, high + 1, key_tile, 0)
+    own = REACH * per_block - 1
+    lax.fori_loop(low, own, key_tile, 0)
+    one_tile(own, True, (t + 1) * span // WAYS)
     dq = (dq_acc[...].T * SCALE).astype(BF16).reshape(sources, 2, STRIP, HEAD_DIM)
     for i, ref in enumerate(dq_refs):
         ref[ms] = dq[:, i]

time: 120 us -> 116 us (0.967); the launches traced: 120 us -> 115 us
  starting transfers between devices: 32 us -> 27.3 us
    all_to_all x1, starting transfers between devices: 16 us -> 11.2 us  [per_device(): dkv = lax.all_to_all(dkv_part, 'qrow', 0, 0)]
where the time goes in v6:
time: 116 us; the launch traced here: 115 us
  blocking collectives  44 us (38%)
  waiting for transfers between devices  31.7 us (27%)
  starting transfers between devices  27.3 us (24%)
  Pallas kernels  11.1 us (10%)
    all_to_all x1, blocking collectives, per_device(): mine = lax.all_to_all(packed, KCOL, 0, 0)  26.2 us
    ppermute x6, waiting for transfers between devices, from_partner(): return lax.ppermute(x, STRIPS, [(d, d ^ s) for d in range(WAYS)])  22.2 us
    all_to_all x1, blocking collectives, per_device(): back = lax.all_to_all(sums, KCOL, 0, 0)  17.9 us
    all_to_all x1, starting transfers between devices, per_device(): dkv = lax.all_to_all(dkv_part, 'qrow', 0, 0)  11.2 us
    ppermute x6, starting transfers between devices, from_partner(): return lax.ppermute(x, STRIPS, [(d, d ^ s) for d in range(WAYS)])  9.78 us
    all_to_all x1, starting transfers between devices, per_device(): keys = lax.all_to_all(spread, 'qrow', 0, 0)  6.27 us
    all_to_all x1, waiting for transfers between devices, per_device(): dkv = lax.all_to_all(dkv_part, 'qrow', 0, 0)  5.34 us
    all_to_all x1, waiting for transfers between devices, per_device(): keys = lax.all_to_all(spread, 'qrow', 0, 0)  4.23 us
  transfers between devices with their start and end apart: 8, of which 6 were waited for; matrix products, arithmetic and copies ran while one was open for 0% of the time, Pallas kernels for 2%

profile of v6, /device:TPU:40, one launch (start us, length us, event | category | flops | bytes accessed | tf_op | source)
XLA Modules:
  0.0 114.9 jit_solution(12287548630904143199)
XLA Ops:
  0.6 2.6 %shard_map.94 = bf16[16,136,128]{2,1,0:T(8,128)(2,1)} custom-call(bf16[128,512]{1,0:T(8,128)(2,1)} %q_ref.1, bf16[128,512]{1,0:T(8,128)(2,1)} %k_ref.1, bf16[128,512]{1,0:T(8,128)(2,1)} %v_ref.1, bf16[128,512]{1,0:T(8,128)(2,1)} %o_ref.1, bf16[128,512]{1,0:T(8,128)(2,1)} %g_ref.1, f32[4,128]{1,0:T(4,128)} %bitcast.3), custom_call_target="tpu_custom_call" | custom-call | tf_op jit(solution)/shard_map/pallas_call | solution.py:271
  3.2 26.2 %all_to_all.20.in_ref = bf16[16,136,128]{2,1,0:T(8,128)(2,1)S(1)} all-to-all(bf16[16,136,128]{2,1,0:T(8,128)(2,1)} %shard_map.94), channel_id=1, replica_groups=mesh['qrow'=16,'kcol_h'=4,'kcol_s'=4] {'kcol_h','kcol_s'}, dimensions={0} | all-to-all | bytes 1114112 | tf_op jit(solution)/shard_map/all_to_all | solution.py:278
  29.4 1.3 %shard_map.95 = (bf16[16,5,64,128]{3,2,1,0:T(8,128)(2,1)}, bf16[16,64,128]{2,1,0:T(8,128)(2,1)S(1)}) custom-call(bf16[16,136,128]{2,1,0:T(8,128)(2,1)S(1)} %all_to_all.20.in_ref), custom_call_target="tpu_custom_call" | custom-call | tf_op jit(solution)/shard_map/pallas_call | solution.py:279
  30.6 0.0 copy-start
  30.6 6.3 %all-to-all-start.1 = ((bf16[16,5,64,128]{3,2,1,0:T(8,128)(2,1)}), bf16[16,5,64,128]{3,2,1,0:T(8,128)(2,1)S(1)}, u32[]{:S(2)}, u32[]{:S(2)}) async-start(bf16[16,5,64,128]{3,2,1,0:T(8,128)(2,1)} %get-tuple-element.13), calls=%async_computation.1 | async-start | bytes 2621440 | tf_op jit(solution)/shard_map/all_to_all | solution.py:286
  36.9 0.7 collective-permute-start.2
  37.6 1.4 %collective-permute-start = (bf16[16,64,128]{2,1,0:T(8,128)(2,1)S(1)}, bf16[16,64,128]{2,1,0:T(8,128)(2,1)S(1)}, u32[]{:S(2)}, u32[]{:S(2)}) collective-permute-start(bf16[16,64,128]{2,1,0:T(8,128)(2,1)S(1)} %get-tuple-element.12.qg0), channel_id=1, source_target_pairs={{0,1},{1,0},{2,3},{3,2},{4,5},{5,4},{6,7},{7,6},{8,9},{9,8},{10,11... | collective-permute-start | bytes 786440 | tf_op jit(solution)/shard_map/ppermute | solution.py:240
  39.1 10.3 %collective-permute-done.2.qg2 = bf16[16,64,128]{2,1,0:T(8,128)(2,1)S(1)} collective-permute-done((bf16[16,64,128]{2,1,0:T(8,128)(2,1)S(1)}, bf16[16,64,128]{2,1,0:T(8,128)(2,1)S(1)}, u32[]{:S(2)}, u32[]{:S(2)}) %collective-permute-start.2) | collective-permute-done | bytes 262176 | tf_op jit(solution)/shard_map/ppermute | solution.py:240
  49.3 4.1 %collective-permute-start.3 = (bf16[16,64,128]{2,1,0:T(8,128)(2,1)S(1)}, bf16[16,64,128]{2,1,0:T(8,128)(2,1)S(1)}, u32[]{:S(2)}, u32[]{:S(2)}) collective-permute-start(bf16[16,64,128]{2,1,0:T(8,128)(2,1)S(1)} %collective-permute-done.2.qg2), channel_id=1, source_target_pairs={{0,1},{1,0},{2,3},{3,2},{4,5},{5,4},{6,7},{7,6},{8,9},{9,8},{10,11... | collective-permute-start | bytes 786440 | tf_op jit(solution)/shard_map/ppermute | solution.py:240
  53.4 0.1 pad_add_fusion.place_ref
  53.5 0.0 collective-permute-done.qg1
  53.5 4.2 %all-to-all-done.1.kv_ref = bf16[16,5,64,128]{3,2,1,0:T(8,128)(2,1)S(1)} async-done(((bf16[16,5,64,128]{3,2,1,0:T(8,128)(2,1)}), bf16[16,5,64,128]{3,2,1,0:T(8,128)(2,1)S(1)}, u32[]{:S(2)}, u32[]{:S(2)}) %all-to-all-start.1) | async-done | bytes 1310752 | tf_op jit(solution)/shard_map/all_to_all | solution.py:286
  57.7 0.0 copy-done
  57.7 2.5 %shard_map.96 = (bf16[16,32,128]{2,1,0:T(8,128)(2,1)S(1)}, bf16[16,32,128]{2,1,0:T(8,128)(2,1)S(1)}, f32[5,512,128]{2,1,0:T(8,128)S(1)}, f32[5,512,128]{2,1,0:T(8,128)S(1)}) custom-call(s32[2]{0:T(128)S(1)} %pad_add_fusion.place_ref, s32[8]{0:T(128)S(1)} %copy-done, bf16[16,136,128]{2,1,0:T(8,128)(2,1)S(1)} %all_to_all.20.in_ref, ...), custom_call_target="tpu_custom_call" | custom-call | tf_op jit(solution)/shard_map/pallas_call | solution.py:248
  60.2 0.0 collective-permute-done.3.qg3
  60.2 3.8 %shard_map.97 = (bf16[16,32,128]{2,1,0:T(8,128)(2,1)S(1)}, bf16[16,32,128]{2,1,0:T(8,128)(2,1)S(1)}, bf16[16,5,64,128]{3,2,1,0:T(8,128)(2,1)}) custom-call(s32[2]{0:T(128)S(1)} %pad_add_fusion.place_ref, s32[8]{0:T(128)S(1)} %copy-done, bf16[16,136,128]{2,1,0:T(8,128)(2,1)S(1)} %all_to_all.20.in_ref, bf16[16,64,128]{2,1,0:T(8,128)(2,1)S(1)} %collective-permute-done.2.qg2, ...), custom_call_target="tpu_custom_call" | custom-call | tf_op jit(solution)/shard_map/pallas_call | solution.py:256
  64.0 11.2 %all-to-all-start.2 = ((bf16[16,5,64,128]{3,2,1,0:T(8,128)(2,1)}), bf16[16,5,64,128]{3,2,1,0:T(8,128)(2,1)S(1)}, u32[]{:S(2)}, u32[]{:S(2)}) async-start(bf16[16,5,64,128]{3,2,1,0:T(8,128)(2,1)} %get-tuple-element.20), calls=%async_computation.2 | async-start | bytes 2621440 | tf_op jit(solution)/shard_map/all_to_all | solution.py:290
  75.2 1.4 %collective-permute-start.1 = (bf16[16,32,128]{2,1,0:T(8,128)(2,1)S(1)}, bf16[16,32,128]{2,1,0:T(8,128)(2,1)S(1)}, u32[]{:S(2)}, u32[]{:S(2)}) collective-permute-start(bf16[16,32,128]{2,1,0:T(8,128)(2,1)S(1)} %get-tuple-element.15), channel_id=1, source_target_pairs={{0,1},{1,0},{2,3},{3,2},{4,5},{5,4},{6,7},{7,6},{8,9},{9,8},{10,11... | collective-permute-start | bytes 393224 | tf_op jit(solution)/shard_map/ppermute | solution.py:240
  76.6 0.7 collective-permute-start.4
  77.3 1.5 %collective-permute-start.5 = (bf16[16,32,128]{2,1,0:T(8,128)(2,1)S(1)}, bf16[16,32,128]{2,1,0:T(8,128)(2,1)S(1)}, u32[]{:S(2)}, u32[]{:S(2)}) collective-permute-start(bf16[16,32,128]{2,1,0:T(8,128)(2,1)S(1)} %get-tuple-element.19), channel_id=1, source_target_pairs={{0,3},{1,2},{2,1},{3,0},{4,7},{5,6},{6,5},{7,4},{8,11},{9,10},{10,... | collective-permute-start | bytes 393224 | tf_op jit(solution)/shard_map/ppermute | solution.py:240
  78.8 2.8 %collective-permute-done.1.dq1 = bf16[16,32,128]{2,1,0:T(8,128)(2,1)S(1)} collective-permute-done((bf16[16,32,128]{2,1,0:T(8,128)(2,1)S(1)}, bf16[16,32,128]{2,1,0:T(8,128)(2,1)S(1)}, u32[]{:S(2)}, u32[]{:S(2)}) %collective-permute-start.1) | collective-permute-done | bytes 131104 | tf_op jit(solution)/shard_map/ppermute | solution.py:240
  81.7 5.2 %collective-permute-done.4.dq2 = bf16[16,32,128]{2,1,0:T(8,128)(2,1)S(1)} collective-permute-done((bf16[16,32,128]{2,1,0:T(8,128)(2,1)S(1)}, bf16[16,32,128]{2,1,0:T(8,128)(2,1)S(1)}, u32[]{:S(2)}, u32[]{:S(2)}) %collective-permute-start.4) | collective-permute-done | bytes 131104 | tf_op jit(solution)/shard_map/ppermute | solution.py:240
  86.8 3.9 %collective-permute-done.5.dq3 = bf16[16,32,128]{2,1,0:T(8,128)(2,1)S(1)} collective-permute-done((bf16[16,32,128]{2,1,0:T(8,128)(2,1)S(1)}, bf16[16,32,128]{2,1,0:T(8,128)(2,1)S(1)}, u32[]{:S(2)}, u32[]{:S(2)}) %collective-permute-start.5) | collective-permute-done | bytes 131104 | tf_op jit(solution)/shard_map/ppermute | solution.py:240
  90.7 5.3 %all-to-all-done.2.dkv_ref = bf16[16,5,64,128]{3,2,1,0:T(8,128)(2,1)S(1)} async-done(((bf16[16,5,64,128]{3,2,1,0:T(8,128)(2,1)}), bf16[16,5,64,128]{3,2,1,0:T(8,128)(2,1)S(1)}, u32[]{:S(2)}, u32[]{:S(2)}) %all-to-all-start.2) | async-done | bytes 1310752 | tf_op jit(solution)/shard_map/all_to_all | solution.py:290
  96.0 0.2 shard_map.98
  96.2 17.9 %all_to_all.21.in_ref = bf16[16,96,128]{2,1,0:T(8,128)(2,1)S(1)} all-to-all(bf16[16,96,128]{2,1,0:T(8,128)(2,1)S(1)} %shard_map.98), channel_id=1, replica_groups=mesh['qrow'=16,'kcol_h'=4,'kcol_s'=4] {'kcol_h','kcol_s'}, dimensions={0} | all-to-all | bytes 786432 | tf_op jit(solution)/shard_map/all_to_all | solution.py:299
  114.1 0.8 shard_map.99
Async XLA Ops:
  30.6 27.1 %copy-start = (s32[8]{0:T(128)S(1)}, s32[8]{0:T(128)}, u32[]{:S(2)}) copy-start(s32[8]{0:T(128)} %lengths_ref.3) | copy-start | bytes 100
  30.6 27.1 %all-to-all-start.1 = ((bf16[16,5,64,128]{3,2,1,0:T(8,128)(2,1)}), bf16[16,5,64,128]{3,2,1,0:T(8,128)(2,1)S(1)}, u32[]{:S(2)}, u32[]{:S(2)}) async-start(bf16[16,5,64,128]{3,2,1,0:T(8,128)(2,1)} %get-tuple-element.13), calls=%async_computation.1 | async-start | bytes 2621440 | tf_op jit(solution)/shard_map/all_to_all | solution.py:286
  36.9 12.4 %collective-permute-start.2 = (bf16[16,64,128]{2,1,0:T(8,128)(2,1)S(1)}, bf16[16,64,128]{2,1,0:T(8,128)(2,1)S(1)}, u32[]{:S(2)}, u32[]{:S(2)}) collective-permute-start(bf16[16,64,128]{2,1,0:T(8,128)(2,1)S(1)} %get-tuple-element.12.qg0), channel_id=1, source_target_pairs={{0,2},{1,3},{2,0},{3,1},{4,6},{5,7},{6,4},{7,5},{8,10},{9,11},{10,... | collective-permute-start | bytes 786440 | tf_op jit(solution)/shard_map/ppermute | solution.py:240
  37.6 15.9 %collective-permute-start = (bf16[16,64,128]{2,1,0:T(8,128)(2,1)S(1)}, bf16[16,64,128]{2,1,0:T(8,128)(2,1)S(1)}, u32[]{:S(2)}, u32[]{:S(2)}) collective-permute-start(bf16[16,64,128]{2,1,0:T(8,128)(2,1)S(1)} %get-tuple-element.12.qg0), channel_id=1, source_target_pairs={{0,1},{1,0},{2,3},{3,2},{4,5},{5,4},{6,7},{7,6},{8,9},{9,8},{10,11... | collective-permute-start | bytes 786440 | tf_op jit(solution)/shard_map/ppermute | solution.py:240
  49.3 10.9 %collective-permute-start.3 = (bf16[16,64,128]{2,1,0:T(8,128)(2,1)S(1)}, bf16[16,64,128]{2,1,0:T(8,128)(2,1)S(1)}, u32[]{:S(2)}, u32[]{:S(2)}) collective-permute-start(bf16[16,64,128]{2,1,0:T(8,128)(2,1)S(1)} %collective-permute-done.2.qg2), channel_id=1, source_target_pairs={{0,1},{1,0},{2,3},{3,2},{4,5},{5,4},{6,7},{7,6},{8,9},{9,8},{10,11... | collective-permute-start | bytes 786440 | tf_op jit(solution)/shard_map/ppermute | solution.py:240
  64.0 32.0 %all-to-all-start.2 = ((bf16[16,5,64,128]{3,2,1,0:T(8,128)(2,1)}), bf16[16,5,64,128]{3,2,1,0:T(8,128)(2,1)S(1)}, u32[]{:S(2)}, u32[]{:S(2)}) async-start(bf16[16,5,64,128]{3,2,1,0:T(8,128)(2,1)} %get-tuple-element.20), calls=%async_computation.2 | async-start | bytes 2621440 | tf_op jit(solution)/shard_map/all_to_all | solution.py:290
  75.2 6.4 %collective-permute-start.1 = (bf16[16,32,128]{2,1,0:T(8,128)(2,1)S(1)}, bf16[16,32,128]{2,1,0:T(8,128)(2,1)S(1)}, u32[]{:S(2)}, u32[]{:S(2)}) collective-permute-start(bf16[16,32,128]{2,1,0:T(8,128)(2,1)S(1)} %get-tuple-element.15), channel_id=1, source_target_pairs={{0,1},{1,0},{2,3},{3,2},{4,5},{5,4},{6,7},{7,6},{8,9},{9,8},{10,11... | collective-permute-start | bytes 393224 | tf_op jit(solution)/shard_map/ppermute | solution.py:240
  76.6 10.2 %collective-permute-start.4 = (bf16[16,32,128]{2,1,0:T(8,128)(2,1)S(1)}, bf16[16,32,128]{2,1,0:T(8,128)(2,1)S(1)}, u32[]{:S(2)}, u32[]{:S(2)}) collective-permute-start(bf16[16,32,128]{2,1,0:T(8,128)(2,1)S(1)} %get-tuple-element.18), channel_id=1, source_target_pairs={{0,2},{1,3},{2,0},{3,1},{4,6},{5,7},{6,4},{7,5},{8,10},{9,11},{10,... | collective-permute-start | bytes 393224 | tf_op jit(solution)/shard_map/ppermute | solution.py:240
  77.3 13.4 %collective-permute-start.5 = (bf16[16,32,128]{2,1,0:T(8,128)(2,1)S(1)}, bf16[16,32,128]{2,1,0:T(8,128)(2,1)S(1)}, u32[]{:S(2)}, u32[]{:S(2)}) collective-permute-start(bf16[16,32,128]{2,1,0:T(8,128)(2,1)S(1)} %get-tuple-element.19), channel_id=1, source_target_pairs={{0,3},{1,2},{2,1},{3,0},{4,7},{5,6},{6,5},{7,4},{8,11},{9,10},{10,... | collective-permute-start | bytes 393224 | tf_op jit(solution)/shard_map/ppermute | solution.py:240
